TPU v7x, 32 devices: a whole 2x2x4 slice. The times are simulated.
32 devices in a mesh: head: 4 (over y, core), blk: 8 (over z, x).
Axes of the slice: x: 2, y: 2, z: 4, core: 2. Of those that a mesh axis runs over, the one named last changes fastest.
Arguments:
- embedded: bfloat16 [4096, 2048], P(('blk', 'head')), may hold values from -10.5 to 10.5
- cotangent: bfloat16 [4096, 2048], P(('blk', 'head')), may hold values from -6 to 6
- doc_lengths: int32 [8], replicated, may hold values from 1 to 1024, 4096 in all
- emb_gain: float32 [2048], replicated, may hold values from 0.25 to 1.75
- emb_bias: float32 [2048], replicated, may hold values from -3 to 3
- attn_gain: float32 [2, 2048], replicated, may hold values from 0.25 to 1.75
- attn_bias: float32 [2, 2048], replicated, may hold values from -3 to 3
- qkv_weight: bfloat16 [2, 2048, 6144], P(None, 'blk', 'head'), may hold values from -0.125 to 0.125
- qv_bias: float32 [2, 16, 2, 128], replicated, may hold values from -4 to 4
- out_weight: bfloat16 [2, 2048, 2048], P(None, 'head', 'blk'), may hold values from -0.5 to 0.5
- out_bias: float32 [2, 2048], replicated, may hold values from -4 to 4
- ffn_gain: float32 [2, 2048], replicated, may hold values from 0.25 to 1.75
- ffn_bias: float32 [2, 2048], replicated, may hold values from -3 to 3
- up_weight: bfloat16 [2, 2048, 8192], P(None, 'blk', 'head'), may hold values from -0.125 to 0.125
- up_bias: float32 [2, 8192], replicated, may hold values from -4 to 4
- down_weight: bfloat16 [2, 8192, 2048], P(None, 'head', 'blk'), may hold values from -0.0625 to 0.0625
- down_bias: float32 [2, 2048], replicated, may hold values from -4 to 4
Outputs:
- hidden_out: float32 [4096, 2048], P(('blk', 'head'))
- embedded_grad: float32 [4096, 2048], P(('blk', 'head'))
- emb_gain_grad: float32 [2048], replicated
- emb_bias_grad: float32 [2048], replicated
- attn_gain_grad: float32 [2, 2048], replicated
- attn_bias_grad: float32 [2, 2048], replicated
- qkv_weight_grad: float32 [2, 2048, 6144], P(None, 'blk', 'head')
- qv_bias_grad: float32 [2, 16, 2, 128], replicated
- out_weight_grad: float32 [2, 2048, 2048], P(None, 'head', 'blk')
- out_bias_grad: float32 [2, 2048], replicated
- ffn_gain_grad: float32 [2, 2048], replicated
- ffn_bias_grad: float32 [2, 2048], replicated
- up_weight_grad: float32 [2, 2048, 8192], P(None, 'blk', 'head')
- up_bias_grad: float32 [2, 8192], replicated
- down_weight_grad: float32 [2, 8192, 2048], P(None, 'head', 'blk')
- down_bias_grad: float32 [2, 2048], replicated
Inputs may be any that keep to these rules, and one draw needn't show every extreme that they name: `doc_lengths`: lengths of the 8 documents laid end to end in the stream, summing to 4096; the longest is exactly 1024.
All inputs are finite; a program needn't handle non-finite values.
Results may differ from a plain program's by a relative error of at most 0.015.
Values may be sent and summed in bfloat16 or wider, within the bound.
A program may use at most 512 MiB of HBM per device.

v0:
```python
from functools import partial

import jax
import jax.numpy as jnp
from jax import lax
from jax.sharding import PartitionSpec as P

D = 2048
H = 16
FF = 8192
LAYERS = 2


norm_eps = 1e-05


def from_behind(block, axis, distance):
    devices = range(lax.axis_size(axis))
    route = [(i - distance, i) for i in devices if i - distance in devices]
    return lax.ppermute(block, axis, route)


def shifted(value, axis, steps):
    count = lax.axis_size(axis)
    pairs = [(source, (source + steps) % count) for source in range(count)]
    return lax.ppermute(value, axis, pairs)


def layer_norm(values, gain_row, shifts):
    average = jnp.mean(values, axis=-1, keepdims=True)
    centered = values - average
    variance = jnp.mean(centered * centered, axis=-1, keepdims=True)
    return centered * lax.rsqrt(variance + norm_eps) * gain_row + shifts


def gelu_tanh(values):
    return (
        0.5
        * values
        * (1.0 + jnp.tanh(0.7978845608028654 * (values + 0.044715 * values * values * values)))
    )


def doc_numbers(positions, doc_starts):
    return jnp.sum((positions[:, None] >= doc_starts[None, :]).astype(jnp.int32), axis=1) - 1


def gather_rows(values):
    return lax.all_gather(values, "head", axis=0, tiled=True)


def sum_rows(values):
    return lax.psum_scatter(values, "head", scatter_dimension=0, tiled=True)


def matmul_tn(left, right):
    return lax.dot_general(
        left, right, (((0,), (0,)), ((), ())), preferred_element_type=jnp.float32
    )


def matmul_nt(left, right):
    return lax.dot_general(
        left, right, (((1,), (1,)), ((), ())), preferred_element_type=jnp.float32
    )


def block_scores(queries, key_rows, slopes, query_pos, key_pos, allowed):
    scale_factor = queries.shape[-1] ** (-0.5)
    raw_scores = (
        jnp.einsum("qhd,khd->hqk", queries, key_rows, preferred_element_type=jnp.float32)
        * scale_factor
    )
    distance = (key_pos[None, :] - query_pos[:, None]).astype(jnp.float32)
    raw_scores = raw_scores + slopes[:, None, None] * distance[None, :, :]
    return jnp.where(allowed[None, :, :], raw_scores, -jnp.inf)


def block_allowed(query_pos, query_doc, doc_starts, cycle_step, group_rows):
    source = (lax.axis_index("blk") - cycle_step) % lax.axis_size("blk")
    key_pos = source * group_rows + jnp.arange(group_rows)
    key_doc = doc_numbers(key_pos, doc_starts)
    allowed = (key_pos[None, :] <= query_pos[:, None]) & (key_doc[None, :] == query_doc[:, None])
    return (key_pos, allowed)


def add_block(current, weights_now, values_now, row_total):
    probs_low = (weights_now / row_total[:, :, None]).astype(jnp.bfloat16)
    return current + jnp.einsum(
        "hqk,khd->qhd", probs_low, values_now, preferred_element_type=jnp.float32
    )


def attend_forward(
    queries, key_rows, value_rows, slopes, query_pos, query_doc, doc_starts, cycle_len
):
    group_rows, heads_local, head_size = queries.shape
    carried = (key_rows, value_rows)
    empty_scores = jnp.full((heads_local, group_rows, group_rows), -jnp.inf, jnp.float32)
    kept_blocks = []
    for cycle_step in range(cycle_len):
        if cycle_step > 0:
            carried = from_behind((carried[0], carried[1]), "blk", 1)
        key_pos, allowed = block_allowed(query_pos, query_doc, doc_starts, cycle_step, group_rows)
        has_keys = jnp.any(allowed)
        scores = lax.cond(
            has_keys,
            partial(block_scores, queries, carried[0], slopes, query_pos, key_pos, allowed),
            lambda: empty_scores,
        )
        kept_blocks.append((scores, carried[1], has_keys))
    row_max = jnp.max(kept_blocks[0][0], axis=2)
    for block in kept_blocks[1:]:
        row_max = jnp.maximum(row_max, jnp.max(block[0], axis=2))
    exp_blocks = [jnp.exp(block[0] - row_max[:, :, None]) for block in kept_blocks]
    row_total = jnp.sum(exp_blocks[0], axis=2)
    for weights_now in exp_blocks[1:]:
        row_total = row_total + jnp.sum(weights_now, axis=2)
    out_wide = jnp.zeros((group_rows, heads_local, head_size), jnp.float32)
    for weights_now, block in zip(exp_blocks, kept_blocks):
        out_wide = lax.cond(
            block[2],
            partial(add_block, weights_now=weights_now, values_now=block[1], row_total=row_total),
            lambda current: current,
            out_wide,
        )
    log_total = row_max + jnp.log(row_total)
    return (out_wide, log_total)


def gradient_update(
    current,
    queries,
    grad_out,
    out_delta,
    log_total,
    key_rows,
    value_rows,
    slopes,
    query_pos,
    key_pos,
    allowed,
):
    grad_q, grad_k, grad_v = current
    scale_factor = queries.shape[-1] ** (-0.5)
    scores = block_scores(queries, key_rows, slopes, query_pos, key_pos, allowed)
    attn_probs = jnp.exp(scores - log_total[:, :, None])
    grad_probs = jnp.einsum(
        "qhd,khd->hqk", grad_out, value_rows, preferred_element_type=jnp.float32
    )
    grad_scores = (attn_probs * (grad_probs - out_delta[:, :, None])).astype(jnp.bfloat16)
    grad_q = grad_q + scale_factor * jnp.einsum(
        "hqk,khd->qhd", grad_scores, key_rows, preferred_element_type=jnp.float32
    )
    grad_k = grad_k + scale_factor * jnp.einsum(
        "hqk,qhd->khd", grad_scores, queries, preferred_element_type=jnp.float32
    )
    grad_v = grad_v + jnp.einsum(
        "hqk,qhd->khd",
        attn_probs.astype(jnp.bfloat16),
        grad_out,
        preferred_element_type=jnp.float32,
    )
    return (grad_q, grad_k, grad_v)


def attend_backward(
    queries,
    key_rows,
    value_rows,
    out_wide,
    log_total,
    grad_out,
    slopes,
    query_pos,
    query_doc,
    doc_starts,
    cycle_len,
):
    group_rows = queries.shape[0]
    out_delta = jnp.einsum("qhd,qhd->hq", grad_out.astype(jnp.float32), out_wide)
    grad_q = jnp.zeros(queries.shape, jnp.float32)
    carried = (
        key_rows,
        value_rows,
        jnp.zeros(key_rows.shape, jnp.float32),
        jnp.zeros(value_rows.shape, jnp.float32),
    )
    for cycle_step in range(cycle_len):
        if cycle_step > 0:
            carried = (
                shifted(carried[0].astype(jnp.float32), "blk", 1).astype(jnp.bfloat16),
                shifted(carried[1].astype(jnp.float32), "blk", 1).astype(jnp.bfloat16),
                shifted(carried[2], "blk", 1),
                shifted(carried[3], "blk", 1),
            )
        key_pos, allowed = block_allowed(query_pos, query_doc, doc_starts, cycle_step, group_rows)

        def update(current):
            return gradient_update(
                current,
                queries,
                grad_out,
                out_delta,
                log_total,
                carried[0],
                carried[1],
                slopes,
                query_pos,
                key_pos,
                allowed,
            )

        grad_q, grad_k, grad_v = lax.cond(
            jnp.any(allowed), update, lambda current: current, (grad_q, carried[2], carried[3])
        )
        carried = (carried[0], carried[1], grad_k, grad_v)
    grad_k, grad_v = (carried[2], carried[3])
    grad_k, grad_v = shifted((grad_k, grad_v), "blk", 1 - cycle_len)
    return (grad_q, grad_k, grad_v)


def body(
    embedded,
    cotangent,
    doc_lengths,
    emb_gain,
    emb_bias,
    attn_gain,
    attn_bias,
    qkv_weight,
    qv_bias,
    out_weight,
    out_bias,
    ffn_gain,
    ffn_bias,
    up_weight,
    up_bias,
    down_weight,
    down_bias,
):
    head_count = lax.axis_size("head")
    blk_count = lax.axis_size("blk")
    head_index = lax.axis_index("head")
    blk_index = lax.axis_index("blk")
    tok_rows = embedded.shape[0]
    group_rows = tok_rows * head_count
    doc_most = min(2 * group_rows, group_rows * blk_count // 2)
    cycle_len = min(blk_count, doc_most // group_rows + 1)
    heads_local = H // head_count
    ff_local = FF // head_count
    doc_starts = jnp.cumsum(doc_lengths) - doc_lengths
    query_pos = blk_index * group_rows + jnp.arange(group_rows)
    query_doc = doc_numbers(query_pos, doc_starts)
    head_ids = head_index * heads_local + jnp.arange(heads_local)
    slopes = jnp.exp2(-8.0 * (head_ids + 1).astype(jnp.float32) / H)
    embedded_wide = embedded.astype(jnp.float32)
    hidden = layer_norm(embedded_wide, emb_gain, emb_bias)
    kept_values = []
    for layer_index in range(LAYERS):
        qkv_cols, out_rows, up_cols, down_rows = (
            lax.all_gather(qkv_weight[layer_index], "blk", axis=0, tiled=True),
            lax.all_gather(out_weight[layer_index], "blk", axis=1, tiled=True),
            lax.all_gather(up_weight[layer_index], "blk", axis=0, tiled=True),
            lax.all_gather(down_weight[layer_index], "blk", axis=1, tiled=True),
        )
        layer_bias = qv_bias[layer_index]
        bias_all = jnp.stack(
            [layer_bias[:, 0], jnp.zeros_like(layer_bias[:, 0]), layer_bias[:, 1]], axis=1
        )
        normed = layer_norm(hidden, attn_gain[layer_index], attn_bias[layer_index]).astype(
            jnp.bfloat16
        )
        qkv_mat, out_mat = (
            lax.all_gather(qkv_cols, "head", axis=1, tiled=True),
            lax.all_gather(out_rows, "head", axis=0, tiled=True),
        )
        projected = (
            jnp.dot(normed, qkv_mat, preferred_element_type=jnp.float32).reshape(tok_rows, H, 3, -1)
            + bias_all
        )
        grouped = lax.all_to_all(
            projected.astype(jnp.bfloat16), "head", split_axis=1, concat_axis=0, tiled=True
        )
        attn_rows = normed
        queries = grouped[:, :, 0]
        key_rows = grouped[:, :, 1]
        value_rows = grouped[:, :, 2]
        out_wide, log_total = attend_forward(
            queries, key_rows, value_rows, slopes, query_pos, query_doc, doc_starts, cycle_len
        )
        context = out_wide.astype(jnp.bfloat16)
        context_used = lax.all_to_all(
            context, "head", split_axis=0, concat_axis=1, tiled=True
        ).reshape(tok_rows, D)
        attn_out = jnp.dot(context_used, out_mat, preferred_element_type=jnp.float32)
        hidden_mid = hidden + (attn_out + out_bias[layer_index])
        ffn_normed = layer_norm(hidden_mid, ffn_gain[layer_index], ffn_bias[layer_index]).astype(
            jnp.bfloat16
        )
        ffn_rows = gather_rows(ffn_normed)
        own_up_bias = lax.dynamic_slice_in_dim(
            up_bias[layer_index], head_index * ff_local, ff_local, 0
        )
        up_pre = jnp.dot(ffn_rows, up_cols, preferred_element_type=jnp.float32) + own_up_bias
        activated = gelu_tanh(up_pre).astype(jnp.bfloat16)
        ffn_out = sum_rows(jnp.dot(activated, down_rows, preferred_element_type=jnp.float32))
        kept_values.append(
            (
                hidden,
                hidden_mid,
                attn_rows,
                qkv_mat,
                out_mat,
                up_cols,
                down_rows,
                queries,
                key_rows,
                value_rows,
                out_wide,
                log_total,
                context_used,
                ffn_rows,
                up_pre,
                activated,
            )
        )
        hidden = hidden_mid + (ffn_out + down_bias[layer_index])
    grad_now = cotangent.astype(jnp.float32)
    collected = [None] * LAYERS
    for layer_index in reversed(range(LAYERS)):
        (
            layer_input,
            hidden_mid,
            attn_rows,
            qkv_mat,
            out_mat,
            up_cols,
            down_rows,
            queries,
            key_rows,
            value_rows,
            out_wide,
            log_total,
            context_used,
            ffn_rows,
            up_pre,
            activated,
        ) = kept_values[layer_index]
        grad_low = grad_now.astype(jnp.bfloat16)
        down_bias_grad = jnp.sum(grad_low.astype(jnp.float32), axis=0)
        grad_rows = gather_rows(grad_low)
        grad_act = matmul_nt(grad_rows, down_rows)
        down_grad = matmul_tn(activated, grad_rows)
        gelu_back = jax.vjp(gelu_tanh, up_pre)[1]
        grad_up = gelu_back(grad_act)[0].astype(jnp.bfloat16)
        up_bias_local = jnp.sum(grad_up.astype(jnp.float32), axis=0)
        up_bias_grad = lax.dynamic_update_slice_in_dim(
            jnp.zeros((FF,), jnp.float32), up_bias_local, head_index * ff_local, 0
        )
        up_grad = matmul_tn(ffn_rows, grad_up)
        grad_ffn_normed = sum_rows(matmul_nt(grad_up, up_cols))
        ffn_back = jax.vjp(layer_norm, hidden_mid, ffn_gain[layer_index], ffn_bias[layer_index])[1]
        grad_mid_part, ffn_gain_grad, ffn_bias_grad = ffn_back(grad_ffn_normed)
        grad_mid = grad_now + grad_mid_part
        attn_low = grad_mid.astype(jnp.bfloat16)
        out_bias_grad = jnp.sum(attn_low.astype(jnp.float32), axis=0)
        grad_context_tok = matmul_nt(attn_low, out_mat).astype(jnp.bfloat16)
        out_grad_full = matmul_tn(context_used, attn_low)
        grad_context = lax.all_to_all(
            grad_context_tok.reshape(tok_rows, H, -1),
            "head",
            split_axis=1,
            concat_axis=0,
            tiled=True,
        )
        grad_q, grad_k, grad_v = attend_backward(
            queries,
            key_rows,
            value_rows,
            out_wide,
            log_total,
            grad_context,
            slopes,
            query_pos,
            query_doc,
            doc_starts,
            cycle_len,
        )
        grad_qkv = jnp.stack([grad_q, grad_k, grad_v], axis=2).astype(jnp.bfloat16)
        grad_tok = lax.all_to_all(
            grad_qkv, "head", split_axis=0, concat_axis=1, tiled=True
        ).reshape(tok_rows, 3 * D)
        qkv_grad_full = matmul_tn(attn_rows, grad_tok)
        grad_normed = matmul_nt(grad_tok, qkv_mat)
        bias_sums = jnp.sum(grad_tok.astype(jnp.float32), axis=0).reshape(H, 3, -1)
        qkv_grad, out_grad = (
            lax.psum_scatter(qkv_grad_full, "head", scatter_dimension=1, tiled=True),
            lax.psum_scatter(out_grad_full, "head", scatter_dimension=0, tiled=True),
        )
        qv_bias_grad = jnp.stack([bias_sums[:, 0], bias_sums[:, 2]], axis=1)
        attn_back = jax.vjp(
            layer_norm, layer_input, attn_gain[layer_index], attn_bias[layer_index]
        )[1]
        grad_in_part, attn_gain_grad, attn_bias_grad = attn_back(grad_normed)
        grad_now = grad_mid + grad_in_part
        collected[layer_index] = (
            qkv_grad,
            out_grad,
            up_grad,
            down_grad,
            attn_gain_grad,
            attn_bias_grad,
            qv_bias_grad,
            out_bias_grad,
            ffn_gain_grad,
            ffn_bias_grad,
            up_bias_grad,
            down_bias_grad,
        )
    emb_back = jax.vjp(layer_norm, embedded_wide, emb_gain, emb_bias)[1]
    embedded_grad, emb_gain_grad, emb_bias_grad = emb_back(grad_now)

    def stacked(member):
        return jnp.stack([collected[layer_index][member] for layer_index in range(LAYERS)])

    qkv_grads, out_grads, up_grads, down_grads = (
        lax.psum_scatter(stacked(0), "blk", scatter_dimension=1, tiled=True),
        lax.psum_scatter(stacked(1), "blk", scatter_dimension=2, tiled=True),
        lax.psum_scatter(stacked(2), "blk", scatter_dimension=1, tiled=True),
        lax.psum_scatter(stacked(3), "blk", scatter_dimension=2, tiled=True),
    )
    (
        emb_gain_sum,
        emb_bias_sum,
        attn_gain_sum,
        attn_bias_sum,
        qv_bias_sum,
        out_bias_sum,
        ffn_gain_sum,
        ffn_bias_sum,
        up_bias_sum,
        down_bias_sum,
    ) = lax.psum(
        (
            emb_gain_grad,
            emb_bias_grad,
            stacked(4),
            stacked(5),
            stacked(6),
            stacked(7),
            stacked(8),
            stacked(9),
            stacked(10),
            stacked(11),
        ),
        ("head", "blk"),
    )
    return (
        hidden,
        embedded_grad,
        emb_gain_sum,
        emb_bias_sum,
        attn_gain_sum,
        attn_bias_sum,
        qkv_grads,
        qv_bias_sum,
        out_grads,
        out_bias_sum,
        ffn_gain_sum,
        ffn_bias_sum,
        up_grads,
        up_bias_sum,
        down_grads,
        down_bias_sum,
    )


def solution(mesh):
    in_specs = (
        P(("blk", "head"), None),
        P(("blk", "head"), None),
        P(),
        P(),
        P(),
        P(),
        P(),
        P(None, "blk", "head"),
        P(),
        P(None, "head", "blk"),
        P(),
        P(),
        P(),
        P(None, "blk", "head"),
        P(),
        P(None, "head", "blk"),
        P(),
    )
    out_specs = (
        P(("blk", "head"), None),
        P(("blk", "head"), None),
        P(),
        P(),
        P(),
        P(),
        P(None, "blk", "head"),
        P(),
        P(None, "head", "blk"),
        P(),
        P(),
        P(),
        P(None, "blk", "head"),
        P(),
        P(None, "head", "blk"),
        P(),
    )
    return jax.shard_map(body, mesh=mesh, in_specs=in_specs, out_specs=out_specs, check_vma=False)
```

profile of v0, /device:TPU:0, one launch (start us, length us, event | category | flops | bytes accessed | tf_op | source)
XLA Modules:
  0.0 4773.7 jit_solution(10042900704382646182)
XLA Ops:
  10.9 101.3 %all-gather.37.cloned.1.call-done = bf16[1,2048,1536]{2,1,0:T(8,128)(2,1)} async-done(((bf16[1,256,1536]{2,1,0:T(8,128)(2,1)}), bf16[1,2048,1536]{2,1,0:T(8,128)(2,1)}) %all-gather.37.cloned.1.call-update) | async-done | bytes 6291472 | tf_op jit(solution)/shard_map/all_gather | solution.py:262
  112.3 51.1 %all-gather.41.cloned.1.call-done = bf16[1,512,2048]{2,1,0:T(8,128)(2,1)} async-done(((bf16[1,512,256]{2,1,0:T(8,128)(2,1)}), bf16[1,512,2048]{2,1,0:T(8,128)(2,1)}) %all-gather.41.cloned.1.call-update) | async-done | bytes 2097168 | tf_op jit(solution)/shard_map/all_gather | solution.py:263
  167.8 150.2 %all-gather.39.cloned.1.call-done = bf16[1,2048,6144]{2,1,0:T(8,128)(2,1)} async-done(((bf16[1,2048,1536]{2,1,0:T(8,128)(2,1)}), bf16[1,2048,6144]{2,1,0:T(8,128)(2,1)}) %all-gather.39.cloned.1.call-update) | async-done | bytes 25165840 | tf_op jit(solution)/shard_map/all_gather | solution.py:275
  341.5 37.1 all-to-all-done
  477.4 65.5 %all-gather.45.cloned.1.call-done = bf16[1,2048,2048]{2,1,0:T(8,128)(2,1)} async-done(((bf16[1,256,2048]{2,1,0:T(8,128)(2,1)}), bf16[1,2048,2048]{2,1,0:T(8,128)(2,1)}) %all-gather.45.cloned.1.call-update) | async-done | bytes 8388624 | tf_op jit(solution)/shard_map/all_gather | solution.py:264
  542.9 22.8 all-gather.29.cloned.1.call-done
  576.2 117.1 %all-gather.47.cloned.1.call-done = bf16[1,2048,2048]{2,1,0:T(8,128)(2,1)} async-done(((bf16[1,2048,256]{2,1,0:T(8,128)(2,1)}), bf16[1,2048,2048]{2,1,0:T(8,128)(2,1)}) %all-gather.47.cloned.1.call-update) | async-done | bytes 8388624 | tf_op jit(solution)/shard_map/all_gather | solution.py:265
  704.9 87.4 %all-gather.49.cloned.1.call-done = bf16[1,2048,1536]{2,1,0:T(8,128)(2,1)} async-done(((bf16[1,256,1536]{2,1,0:T(8,128)(2,1)}), bf16[1,2048,1536]{2,1,0:T(8,128)(2,1)}) %all-gather.49.cloned.1.call-update) | async-done | bytes 6291472 | tf_op jit(solution)/shard_map/all_gather | solution.py:262
  792.4 50.5 %all-gather.53.cloned.1.call-done = bf16[1,512,2048]{2,1,0:T(8,128)(2,1)} async-done(((bf16[1,512,256]{2,1,0:T(8,128)(2,1)}), bf16[1,512,2048]{2,1,0:T(8,128)(2,1)}) %all-gather.53.cloned.1.call-update) | async-done | bytes 2097168 | tf_op jit(solution)/shard_map/all_gather | solution.py:263
  844.0 44.7 reduce-scatter.13.cloned.1.call-done
  890.4 154.7 %all-gather.51.cloned.1.call-done = bf16[1,2048,6144]{2,1,0:T(8,128)(2,1)} async-done(((bf16[1,2048,1536]{2,1,0:T(8,128)(2,1)}), bf16[1,2048,6144]{2,1,0:T(8,128)(2,1)}) %all-gather.51.cloned.1.call-update) | async-done | bytes 25165840 | tf_op jit(solution)/shard_map/all_gather | solution.py:275
  1063.8 39.8 all_to_all.132
  1195.1 73.0 %all-gather.57.cloned.1.call-done = bf16[1,2048,2048]{2,1,0:T(8,128)(2,1)} async-done(((bf16[1,256,2048]{2,1,0:T(8,128)(2,1)}), bf16[1,2048,2048]{2,1,0:T(8,128)(2,1)}) %all-gather.57.cloned.1.call-update) | async-done | bytes 8388624 | tf_op jit(solution)/shard_map/all_gather | solution.py:264
  1268.1 22.8 all-gather.31.cloned.1.call-done
  1314.9 127.4 %all-gather.59.cloned.1.call-done = bf16[1,2048,2048]{2,1,0:T(8,128)(2,1)} async-done(((bf16[1,2048,256]{2,1,0:T(8,128)(2,1)}), bf16[1,2048,2048]{2,1,0:T(8,128)(2,1)}) %all-gather.59.cloned.1.call-update) | async-done | bytes 8388624 | tf_op jit(solution)/shard_map/all_gather | solution.py:265
  1474.4 30.3 reduce-scatter.17.cloned.1.call-done
  1507.0 44.7 reduce-scatter.15.cloned.1.call-done
  1596.8 22.9 collective-permute-done.8
  1771.5 22.8 all_to_all.134
  1817.8 30.6 all-gather.35.cloned.1.call-done
  1881.8 33.5 reduce-scatter.19.cloned.1.call-done
  1997.0 23.0 collective-permute-done.18
  2170.2 22.6 all_to_all.135
  2197.7 35.1 fusion.205
  2341.2 170.4 %reduce-scatter.23.cloned.1.call-done = f32[2048,1536]{1,0:T(8,128)} async-done(((f32[2048,6144]{1,0:T(8,128)}), f32[2048,1536]{1,0:T(8,128)}) %reduce-scatter.23.cloned.1.call-update) | async-done | bytes 12582928 | tf_op jit(solution)/shard_map/reduce_scatter | solution.py:398
  2511.6 335.2 %reduce-scatter.21.cloned.1.call-done = f32[2048,1536]{1,0:T(8,128)} async-done(((f32[2048,6144]{1,0:T(8,128)}), f32[2048,1536]{1,0:T(8,128)}) %reduce-scatter.21.cloned.1.call-update) | async-done | bytes 12582928 | tf_op jit(solution)/shard_map/reduce_scatter | solution.py:398
  2865.7 115.3 %all-reduce.6.cloned.1.call-done = (f32[2048]{0:T(1024)}, f32[2048]{0:T(1024)}, f32[2,2048]{1,0:T(2,128)}, f32[2,2048]{1,0:T(2,128)}, f32[2,16,2,128]{3,1,2,0:T(...) async-done(((f32[2048]{0:T(1024)}, f32[2048]{0:T(1024)}, f32[2,2048]{1,0:T(2,128)}, f32[2,2048]{1,0:T(2,128)}, ...) | async-done | bytes 147472 | tf_op jit(solution)/shard_map/psum | solution.py:444
  2982.5 127.2 %all-reduce.4.cloned.1.call-done = f32[2,8192]{1,0:T(2,128)} async-done(((f32[2,8192]{1,0:T(2,128)}), f32[2,8192]{1,0:T(2,128)}) %all-reduce.4.cloned.1.call-update) | async-done | bytes 65552 | tf_op jit(solution)/shard_map/psum | solution.py:444
  3109.6 153.2 %reduce-scatter.31.cloned.1.call-done = f32[2,512,256]{2,1,0:T(8,128)} async-done(((f32[2,512,2048]{2,1,0:T(8,128)}), f32[2,512,256]{2,1,0:T(8,128)}) %reduce-scatter.31.cloned.1.call-update) | async-done | bytes 1048592 | tf_op jit(solution)/shard_map/reduce_scatter | solution.py:429
  3262.8 542.1 %reduce-scatter.33.cloned.1.call-done = f32[2,256,2048]{2,1,0:T(8,128)} async-done(((f32[2,2048,2048]{2,1,0:T(8,128)}), f32[2,256,2048]{2,1,0:T(8,128)}) %reduce-scatter.33.cloned.1.call-update) | async-done | bytes 4194320 | tf_op jit(solution)/shard_map/reduce_scatter | solution.py:430
  3804.9 542.2 %reduce-scatter.35.cloned.1.call-done = f32[2,2048,256]{2,1,0:T(8,128)} async-done(((f32[2,2048,2048]{2,1,0:T(8,128)}), f32[2,2048,256]{2,1,0:T(8,128)}) %reduce-scatter.35.cloned.1.call-update) | async-done | bytes 4194320 | tf_op jit(solution)/shard_map/reduce_scatter | solution.py:431
  4347.1 407.3 %reduce-scatter.25.cloned.1.call-done = f32[2,256,1536]{2,1,0:T(8,128)} async-done(((f32[2,2048,1536]{2,1,0:T(8,128)}), f32[2,256,1536]{2,1,0:T(8,128)}) %reduce-scatter.25.cloned.1.call-update) | async-done | bytes 3145744 | tf_op jit(solution)/shard_map/reduce_scatter | solution.py:428
  (562 shorter events, 1012.8 us)
Async XLA Ops:
  7.2 105.0 %all-gather.37.cloned.1.call-start = ((), (), s32[]{:S(2)}) async-start(), calls=%async_computation.37 | async-start | bytes 7077888 | tf_op jit(solution)/shard_map/all_gather | solution.py:262
  9.9 153.5 %all-gather.41.cloned.1.call-start = ((), (), s32[]{:S(2)}) async-start(), calls=%async_computation.39 | async-start | bytes 2359296 | tf_op jit(solution)/shard_map/all_gather | solution.py:263
  10.8 307.1 %all-gather.39.cloned.1.call-start = ((), (), s32[]{:S(2)}) async-start(), calls=%async_computation.38 | async-start | bytes 31457280 | tf_op jit(solution)/shard_map/all_gather | solution.py:275
  112.2 353.9 %all-gather.43.cloned.1.call-start = ((), (), s32[]{:S(2)}) async-start(), calls=%async_computation.40 | async-start | bytes 10485760 | tf_op jit(solution)/shard_map/all_gather | solution.py:276
  163.4 379.4 %all-gather.45.cloned.1.call-start = ((), (), s32[]{:S(2)}) async-start(), calls=%async_computation.41 | async-start | bytes 9437184 | tf_op jit(solution)/shard_map/all_gather | solution.py:264
  455.2 110.5 %all-gather.29.cloned.1.call-start = ((), (), s32[]{:S(2)}) async-start(), calls=%async_computation.20 | async-start | bytes 2621440 | tf_op jit(solution)/shard_map/all_gather | solution.py:49
  472.7 220.6 %all-gather.47.cloned.1.call-start = ((), (), s32[]{:S(2)}) async-start(), calls=%async_computation.42 | async-start | bytes 9437184 | tf_op jit(solution)/shard_map/all_gather | solution.py:265
  475.7 316.6 %all-gather.49.cloned.1.call-start = ((), (), s32[]{:S(2)}) async-start(), calls=%async_computation.43 | async-start | bytes 7077888 | tf_op jit(solution)/shard_map/all_gather | solution.py:262
  476.5 366.4 %all-gather.53.cloned.1.call-start = ((), (), s32[]{:S(2)}) async-start(), calls=%async_computation.45 | async-start | bytes 2359296 | tf_op jit(solution)/shard_map/all_gather | solution.py:263
  477.3 411.4 %reduce-scatter.13.cloned.1.call-start = ((), (), s32[]{:S(2)}) async-start(), calls=%async_computation.21 | async-start | bytes 5242880 | tf_op jit(solution)/shard_map/reduce_scatter | solution.py:53
  704.9 340.2 %all-gather.51.cloned.1.call-start = ((), (), s32[]{:S(2)}) async-start(), calls=%async_computation.44 | async-start | bytes 31457280 | tf_op jit(solution)/shard_map/all_gather | solution.py:275
  792.4 394.9 %all-gather.55.cloned.1.call-start = ((), (), s32[]{:S(2)}) async-start(), calls=%async_computation.46 | async-start | bytes 10485760 | tf_op jit(solution)/shard_map/all_gather | solution.py:276
  843.0 425.2 %all-gather.57.cloned.1.call-start = ((), (), s32[]{:S(2)}) async-start(), calls=%async_computation.47 | async-start | bytes 9437184 | tf_op jit(solution)/shard_map/all_gather | solution.py:264
  843.7 447.2 %all-gather.31.cloned.1.call-start = ((), (), s32[]{:S(2)}) async-start(), calls=%async_computation.22 | async-start | bytes 2621440 | tf_op jit(solution)/shard_map/all_gather | solution.py:49
  1193.5 121.4 %all-gather.33.cloned.1.call-start = ((), (), s32[]{:S(2)}) async-start(), calls=%async_computation.24 | async-start | bytes 2621440 | tf_op jit(solution)/shard_map/all_gather | solution.py:49
  1194.1 248.3 %all-gather.59.cloned.1.call-start = ((), (), s32[]{:S(2)}) async-start(), calls=%async_computation.48 | async-start | bytes 9437184 | tf_op jit(solution)/shard_map/all_gather | solution.py:265
  1194.7 310.1 %reduce-scatter.17.cloned.1.call-start = ((), (), s32[]{:S(2)}) async-start(), calls=%async_computation.25 | async-start | bytes 5242880 | tf_op jit(solution)/shard_map/reduce_scatter | solution.py:53
  1461.9 89.9 %reduce-scatter.15.cloned.1.call-start = ((), (), s32[]{:S(2)}) async-start(), calls=%async_computation.23 | async-start | bytes 5242880 | tf_op jit(solution)/shard_map/reduce_scatter | solution.py:53
  1568.1 280.3 %all-gather.35.cloned.1.call-start = ((), (), s32[]{:S(2)}) async-start(), calls=%async_computation.26 | async-start | bytes 2621440 | tf_op jit(solution)/shard_map/all_gather | solution.py:49
  1595.3 67.8 %collective-permute-start.11 = (bf16[512,4,128]{2,0,1:T(8,128)(2,1)}, bf16[512,4,128]{2,0,1:T(8,128)(2,1)S(1)}, u32[]{:S(2)}, u32[]{:S(2)}) collective-permute-start(bf16[512,4,128]{2,0,1:T(8,128)(2,1)} %get-tuple-element.960), channel_id=1, source_target_pairs={{0,1},{1,2},{2,3},{3,4},{4,5},{5,6},{6,7},{7,0},{8,9},{9,10},{10,1... | collective-permute-start | bytes 1572872 | tf_op jit(solution)/shard_map/ppermute | solution.py:26
  1817.8 97.5 %reduce-scatter.19.cloned.1.call-start = ((), (), s32[]{:S(2)}) async-start(), calls=%async_computation.27 | async-start | bytes 5242880 | tf_op jit(solution)/shard_map/reduce_scatter | solution.py:53
  1870.6 391.4 %reduce-scatter.29.cloned.1.call-start = ((), (), s32[]{:S(2)}) async-start(), calls=%async_computation.32 | async-start | bytes 20971520 | tf_op jit(solution)/shard_map/reduce_scatter | solution.py:399
  1881.8 380.3 %reduce-scatter.27.cloned.1.call-start = ((), (), s32[]{:S(2)}) async-start(), calls=%async_computation.31 | async-start | bytes 20971520 | tf_op jit(solution)/shard_map/reduce_scatter | solution.py:399
  1931.3 580.2 %reduce-scatter.23.cloned.1.call-start = ((), (), s32[]{:S(2)}) async-start(), calls=%async_computation.29 | async-start | bytes 62914560 | tf_op jit(solution)/shard_map/reduce_scatter | solution.py:398
  1967.4 879.4 %reduce-scatter.21.cloned.1.call-start = ((), (), s32[]{:S(2)}) async-start(), calls=%async_computation.28 | async-start | bytes 62914560 | tf_op jit(solution)/shard_map/reduce_scatter | solution.py:398
  1995.6 68.1 %collective-permute-start.21 = (bf16[512,4,128]{2,0,1:T(8,128)(2,1)}, bf16[512,4,128]{2,0,1:T(8,128)(2,1)S(1)}, u32[]{:S(2)}, u32[]{:S(2)}) collective-permute-start(bf16[512,4,128]{2,0,1:T(8,128)(2,1)} %copy-done.46), channel_id=1, source_target_pairs={{0,1},{1,2},{2,3},{3,4},{4,5},{5,6},{6,7},{7,0},{8,9},{9,10},{10,1... | collective-permute-start | bytes 1572872 | tf_op jit(solution)/shard_map/ppermute | solution.py:26
  2232.8 748.2 %all-reduce.6.cloned.1.call-start = ((), (), s32[]{:S(2)}) async-start(), calls=%async_computation.49 | async-start | bytes 294912 | tf_op jit(solution)/shard_map/psum | solution.py:444
  2261.2 848.5 %all-reduce.4.cloned.1.call-start = ((), (), s32[]{:S(2)}) async-start(), calls=%async_computation.35 | async-start | bytes 131072 | tf_op jit(solution)/shard_map/psum | solution.py:444
  2261.9 1000.9 %reduce-scatter.31.cloned.1.call-start = ((), (), s32[]{:S(2)}) async-start(), calls=%async_computation.33 | async-start | bytes 9437184 | tf_op jit(solution)/shard_map/reduce_scatter | solution.py:429
  2270.0 1534.8 %reduce-scatter.33.cloned.1.call-start = ((), (), s32[]{:S(2)}) async-start(), calls=%async_computation.34 | async-start | bytes 37748736 | tf_op jit(solution)/shard_map/reduce_scatter | solution.py:430
  2304.9 2042.2 %reduce-scatter.35.cloned.1.call-start = ((), (), s32[]{:S(2)}) async-start(), calls=%async_computation.36 | async-start | bytes 37748736 | tf_op jit(solution)/shard_map/reduce_scatter | solution.py:431
  2341.2 2413.2 %reduce-scatter.25.cloned.1.call-start = ((), (), s32[]{:S(2)}) async-start(), calls=%async_computation.30 | async-start | bytes 28311552 | tf_op jit(solution)/shard_map/reduce_scatter | solution.py:428
  (138 other events, 7975.2 us)
Sparse Core Ops, SparseCore 0:
  10.8 101.3 all-gather.36
  114.8 48.5 all-gather.40
  165.0 152.9 all-gather.38
  319.4 75.1 all-gather.42
  396.5 146.3 all-gather.44
  544.9 20.7 all-gather.28
  568.3 124.9 all-gather.46
  695.4 96.8 all-gather.48
  794.4 48.5 all-gather.52
  845.9 42.7 reduce-scatter.12
  890.3 154.7 all-gather.50
  1046.5 75.1 all-gather.54
  1124.3 143.7 all-gather.56
  1270.1 20.7 all-gather.30
  1292.3 22.5 all-gather.32
  1317.4 124.9 all-gather.58
  1462.0 42.7 reduce-scatter.16
  1507.2 44.5 reduce-scatter.14
  1817.9 30.4 all-gather.34
  1870.7 44.5 reduce-scatter.18
  1917.9 130.6 reduce-scatter.28
  2051.2 125.0 reduce-scatter.26
  2178.8 332.7 reduce-scatter.22
  2514.0 332.7 reduce-scatter.20
  2854.4 126.6 all-reduce.5
  2987.1 122.5 all-reduce.3
  3113.7 149.0 reduce-scatter.30
  3267.1 537.6 reduce-scatter.32
  3809.2 537.8 reduce-scatter.34
  4351.4 402.9 reduce-scatter.24
where the time goes:
time: 4790 us; the launch traced here: 4770 us
  waiting for transfers between devices  4000 us (84%)
  matrix products  315 us (7%)
  other arithmetic  128 us (3%)
  starting transfers between devices  122 us (3%)
  blocking collectives  96.4 us (2%)
  local copies, waits for them, and re-layouts  90.1 us (2%)
    reduce_scatter x1, waiting for transfers between devices, body(): lax.psum_scatter(stacked(3), 'blk', scatter_dimension=2, tiled=True)  542 us
    reduce_scatter x1, waiting for transfers between devices, body(): lax.psum_scatter(stacked(2), 'blk', scatter_dimension=1, tiled=True)  542 us
    reduce_scatter x2, waiting for transfers between devices, body(): lax.psum_scatter(qkv_grad_full, 'head', scatter_dimension=1, tiled=True)  506 us
    reduce_scatter x1, waiting for transfers between devices, body(): lax.psum_scatter(stacked(0), 'blk', scatter_dimension=1, tiled=True)  407 us
    all_gather x2, waiting for transfers between devices, body(): lax.all_gather(qkv_cols, 'head', axis=1, tiled=True)  305 us
    ppermute x20, waiting for transfers between devices, shifted(): return lax.ppermute(value, axis, pairs)  302 us
    all_gather x2, waiting for transfers between devices, body(): lax.all_gather(down_weight[layer_index], 'blk', axis=1, tiled=True)  244 us
    psum x2, waiting for transfers between devices, body(): lax.psum((emb_gain_grad, emb_bias_grad, stacked(4), stacked(5), stacked(6...  242 us
  transfers between devices with their start and end apart: 62, of which 53 were waited for; matrix products, arithmetic and copies ran while one was open for 9% of the time, Pallas kernels for 0%

commit v1 on v0

v1 whole, which is shorter than its diff:
```python
from functools import partial

import jax
import jax.numpy as jnp
from jax import lax
from jax.experimental import pallas as pl
from jax.experimental.pallas import tpu as pltpu
from jax.sharding import PartitionSpec as P

D = 2048
H = 16
HD = 128
FF = 8192
LAYERS = 2

norm_eps = 1e-05
bf16 = jnp.bfloat16
f32 = jnp.float32


def layer_norm(values, gain_row, shifts):
    average = jnp.mean(values, axis=-1, keepdims=True)
    centered = values - average
    variance = jnp.mean(centered * centered, axis=-1, keepdims=True)
    return centered * lax.rsqrt(variance + norm_eps) * gain_row + shifts


def gelu_tanh(values):
    return (
        0.5
        * values
        * (1.0 + jnp.tanh(0.7978845608028654 * (values + 0.044715 * values * values * values)))
    )


def dot(left, right, left_dim, right_dim):
    return lax.dot_general(
        left, right, (((left_dim,), (right_dim,)), ((), ())), preferred_element_type=f32
    )


def ring_ok():
    return lax.axis_size("blk") == 8


def z_next(value, step):
    pairs = [(z * 2 + x, (z + step) % 4 * 2 + x) for z in range(4) for x in range(2)]
    return lax.ppermute(value, "blk", pairs)


def x_swap(value):
    return lax.ppermute(value, "blk", [(i, i ^ 1) for i in range(8)])


def to_relative(values):
    if not ring_ok():
        return values
    index = lax.axis_index("blk")
    z, x = index // 2, index % 2
    width = values.shape[-1] // 8
    parts = [values[..., i * width : (i + 1) * width] for i in range(8)]
    swapped = [parts[i ^ 1] for i in range(8)]
    mine = jnp.where(x == 0, jnp.concatenate(parts, -1), jnp.concatenate(swapped, -1))
    twice = jnp.concatenate([mine, mine], -1)
    return lax.dynamic_slice_in_dim(twice, z * 2 * width, 8 * width, values.ndim - 1)


def to_absolute(values):
    if not ring_ok():
        return values
    index = lax.axis_index("blk")
    z, x = index // 2, index % 2
    width = values.shape[-1] // 8
    twice = jnp.concatenate([values, values], -1)
    turned = lax.dynamic_slice_in_dim(twice, (4 - z) % 4 * 2 * width, 8 * width, values.ndim - 1)
    parts = [turned[..., i * width : (i + 1) * width] for i in range(8)]
    swapped = [parts[i ^ 1] for i in range(8)]
    return jnp.where(x == 0, turned, jnp.concatenate(swapped, -1))


def gather_blocks(shard, axis):
    if not ring_ok():
        return lax.all_gather(shard, "blk", axis=axis, tiled=True)
    held = [shard]
    for _ in range(3):
        held.append(z_next(held[-1], -1))
    pieces = []
    for piece in held:
        pieces += [piece, x_swap(piece)]
    return jnp.concatenate(pieces, axis)


def sum_blocks(piece_of, axis):
    if not ring_ok():
        whole = jnp.concatenate([piece_of(i) for i in range(lax.axis_size("blk"))], axis)
        return lax.psum_scatter(
            whole.astype(bf16), "blk", scatter_dimension=axis, tiled=True
        ).astype(f32)
    total = None
    for k in (3, 2, 1, 0):
        came = x_swap(piece_of(2 * k + 1).astype(bf16))
        mine = piece_of(2 * k).astype(f32) + came.astype(f32)
        if total is not None:
            mine = mine + total.astype(f32)
        if k > 0:
            total = z_next(mine.astype(bf16), 1)
    return mine


def butterfly(values, axis):
    distance = 1
    while distance < lax.axis_size(axis):
        pairs = [(i, i ^ distance) for i in range(lax.axis_size(axis))]
        values = values + lax.ppermute(values, axis, pairs)
        distance *= 2
    return values


def from_behind(block, distance):
    count = lax.axis_size("blk")
    return lax.ppermute(block, "blk", [(i, i + distance) for i in range(count - distance)])


def to_behind(block, distance):
    count = lax.axis_size("blk")
    return lax.ppermute(block, "blk", [(i + distance, i) for i in range(count - distance)])


def gather_rows(values):
    return lax.all_gather(values, "head", axis=0, tiled=True)


def sum_rows(values):
    return lax.psum_scatter(
        values.astype(bf16), "head", scatter_dimension=0, tiled=True
    ).astype(f32)


def key_parts(own_ref, near_ref, far_ref):
    keys = [far_ref[:, :HD], near_ref[:, :HD], own_ref[:, HD : 2 * HD]]
    values = [far_ref[:, HD:], near_ref[:, HD:], own_ref[:, 2 * HD :]]
    return keys, values


def softmax_parts(slope, start_row, queries, keys):
    rows = queries.shape[0]
    scale = HD ** (-0.5)
    query_at = lax.broadcasted_iota(jnp.int32, (rows, rows), 1)
    parts = []
    for i, key in enumerate(keys):
        key_at = lax.broadcasted_iota(jnp.int32, (rows, rows), 0) + (i - 2) * rows
        scores = dot(key, queries, 1, 1) * scale
        scores = scores + slope * (key_at - query_at).astype(f32)
        allowed = (key_at <= query_at) & (key_at >= start_row)
        parts.append(jnp.where(allowed, scores, -jnp.inf))
    top = jnp.maximum(
        jnp.maximum(jnp.max(parts[0], 0, keepdims=True), jnp.max(parts[1], 0, keepdims=True)),
        jnp.max(parts[2], 0, keepdims=True),
    )
    parts = [jnp.exp(part - top) for part in parts]
    total = sum(jnp.sum(part, 0, keepdims=True) for part in parts)
    share = 1.0 / total
    return [part * share for part in parts]


def attend_kernel(slope_ref, start_ref, own_ref, near_ref, far_ref, out_ref):
    slope = slope_ref[pl.program_id(0)]
    keys, values = key_parts(own_ref, near_ref, far_ref)
    probs = softmax_parts(slope, start_ref[0:1, :], own_ref[:, :HD], keys)
    out = sum(dot(p.astype(bf16), v, 0, 0) for p, v in zip(probs, values))
    out_ref[...] = out.astype(out_ref.dtype)


def attend_back_kernel(
    slope_ref, start_ref, own_ref, near_ref, far_ref, grad_ref, own_out, near_out, far_out
):
    slope = slope_ref[pl.program_id(0)]
    scale = HD ** (-0.5)
    keys, values = key_parts(own_ref, near_ref, far_ref)
    queries = own_ref[:, :HD]
    grad = grad_ref[...]
    probs = softmax_parts(slope, start_ref[0:1, :], queries, keys)
    back = [dot(v, grad, 1, 1) for v in values]
    delta = sum(jnp.sum(p * b, 0, keepdims=True) for p, b in zip(probs, back))
    score_grads = [(p * (b - delta)).astype(bf16) for p, b in zip(probs, back)]
    grad_q = sum(dot(s, k, 0, 0) for s, k in zip(score_grads, keys))
    grad_k = [dot(s, queries, 1, 0) * scale for s in score_grads]
    grad_v = [dot(p.astype(bf16), grad, 1, 0) for p in probs]
    far_out[:, :HD] = grad_k[0].astype(bf16)
    far_out[:, HD:] = grad_v[0].astype(bf16)
    near_out[:, :HD] = grad_k[1].astype(bf16)
    near_out[:, HD:] = grad_v[1].astype(bf16)
    own_out[:, :HD] = grad_q * scale
    own_out[:, HD : 2 * HD] = grad_k[2]
    own_out[:, 2 * HD :] = grad_v[2]


def join_kernel(own_ref, near_ref, far_ref, out_ref):
    out_ref[:, :HD] = own_ref[:, :HD].astype(bf16)
    both = own_ref[:, HD:] + (near_ref[...].astype(f32) + far_ref[...].astype(f32))
    out_ref[:, HD:] = both.astype(bf16)


def head_block(rows, width):
    return pl.BlockSpec((rows, width), lambda h: (0, h))


def attention_specs(rows):
    return [
        pl.BlockSpec(memory_space=pltpu.SMEM),
        pl.BlockSpec((8, rows), lambda h: (0, 0)),
        head_block(rows, 3 * HD),
        head_block(rows, 2 * HD),
        head_block(rows, 2 * HD),
    ]


def attend(slopes, start_rows, own, near, far):
    rows, heads = own.shape[0], own.shape[1] // (3 * HD)
    return pl.pallas_call(
        attend_kernel,
        grid=(heads,),
        in_specs=attention_specs(rows),
        out_specs=head_block(rows, HD),
        out_shape=jax.ShapeDtypeStruct((rows, heads * HD), bf16),
        cost_estimate=pl.CostEstimate(
            flops=heads * 12 * rows * rows * HD,
            bytes_accessed=rows * heads * HD * 16,
            transcendentals=heads * 3 * rows * rows,
        ),
        name="attend",
    )(slopes, start_rows, own, near, far)


def attend_back(slopes, start_rows, own, near, far, grad):
    rows, heads = own.shape[0], own.shape[1] // (3 * HD)
    return pl.pallas_call(
        attend_back_kernel,
        grid=(heads,),
        in_specs=attention_specs(rows) + [head_block(rows, HD)],
        out_specs=[head_block(rows, 3 * HD), head_block(rows, 2 * HD), head_block(rows, 2 * HD)],
        out_shape=[
            jax.ShapeDtypeStruct((rows, heads * 3 * HD), f32),
            jax.ShapeDtypeStruct((rows, heads * 2 * HD), bf16),
            jax.ShapeDtypeStruct((rows, heads * 2 * HD), bf16),
        ],
        cost_estimate=pl.CostEstimate(
            flops=heads * 30 * rows * rows * HD,
            bytes_accessed=rows * heads * HD * 32,
            transcendentals=heads * 3 * rows * rows,
        ),
        name="attend_back",
    )(slopes, start_rows, own, near, far, grad)


def join_grads(own, near, far):
    rows, heads = own.shape[0], own.shape[1] // (3 * HD)
    return pl.pallas_call(
        join_kernel,
        grid=(heads,),
        in_specs=[head_block(rows, 3 * HD), head_block(rows, 2 * HD), head_block(rows, 2 * HD)],
        out_specs=head_block(rows, 3 * HD),
        out_shape=jax.ShapeDtypeStruct(own.shape, bf16),
        cost_estimate=pl.CostEstimate(
            flops=own.size * 2, bytes_accessed=own.size * 9, transcendentals=0
        ),
        name="join_grads",
    )(own, near, far)


def body(
    embedded,
    cotangent,
    doc_lengths,
    emb_gain,
    emb_bias,
    attn_gain,
    attn_bias,
    qkv_weight,
    qv_bias,
    out_weight,
    out_bias,
    ffn_gain,
    ffn_bias,
    up_weight,
    up_bias,
    down_weight,
    down_bias,
):
    head_count = lax.axis_size("head")
    head_index = lax.axis_index("head")
    blk_index = lax.axis_index("blk")
    group_rows = embedded.shape[0] * head_count
    heads_local = H // head_count
    ff_local = FF // head_count
    block = D // lax.axis_size("blk")

    doc_starts = jnp.cumsum(doc_lengths) - doc_lengths
    query_pos = blk_index * group_rows + jnp.arange(group_rows, dtype=jnp.int32)
    begun = doc_starts[None, :] <= query_pos[:, None]
    own_start = jnp.max(jnp.where(begun, doc_starts[None, :], 0), axis=1)
    start_rows = jnp.broadcast_to(
        (own_start - blk_index * group_rows).astype(jnp.int32)[None, :], (8, group_rows)
    )
    head_ids = head_index * heads_local + jnp.arange(heads_local)
    slopes = jnp.exp2(-8.0 * (head_ids + 1).astype(f32) / H)

    matrices = []
    for layer in range(LAYERS):
        matrices.append(
            (
                gather_blocks(qkv_weight[layer], 0),
                gather_blocks(out_weight[layer], 1),
                gather_blocks(up_weight[layer], 0),
                gather_blocks(down_weight[layer], 1),
            )
        )

    rows_in = jnp.stack([emb_gain, emb_bias])
    vectors = to_relative(
        jnp.concatenate(
            [rows_in, attn_gain, attn_bias, out_bias, ffn_gain, ffn_bias, down_bias], axis=0
        )
    )
    emb_gain, emb_bias = vectors[0], vectors[1]
    attn_gain, attn_bias, out_bias, ffn_gain, ffn_bias, down_bias = (
        vectors[2 + LAYERS * i : 2 + LAYERS * (i + 1)] for i in range(6)
    )
    embedded_wide = to_relative(embedded).astype(f32)
    grad_now = to_relative(cotangent).astype(f32)

    hidden = layer_norm(embedded_wide, emb_gain, emb_bias)
    kept_values = []
    for layer in range(LAYERS):
        qkv_mat, out_mat, up_mat, down_mat = matrices[layer]
        zeros = jnp.zeros_like(qv_bias[layer][:, 0])
        bias_all = jnp.stack([qv_bias[layer][:, 0], zeros, qv_bias[layer][:, 1]], axis=1)
        own_bias = lax.dynamic_slice_in_dim(
            bias_all.reshape(-1), head_index * heads_local * 3 * HD, heads_local * 3 * HD, 0
        )
        normed = layer_norm(hidden, attn_gain[layer], attn_bias[layer]).astype(bf16)
        normed_rows = gather_rows(normed)
        own = (dot(normed_rows, qkv_mat, 1, 0) + own_bias).astype(bf16)
        sent = jnp.concatenate(
            [own[:, (3 * h + 1) * HD : (3 * h + 3) * HD] for h in range(heads_local)], axis=1
        )
        near, far = from_behind(sent, 1), from_behind(sent, 2)
        context = attend(slopes, start_rows, own, near, far)
        attn_out = sum_rows(dot(context, out_mat, 1, 0))
        hidden_mid = hidden + (attn_out + out_bias[layer])
        ffn_normed = layer_norm(hidden_mid, ffn_gain[layer], ffn_bias[layer]).astype(bf16)
        ffn_rows = gather_rows(ffn_normed)
        own_up_bias = lax.dynamic_slice_in_dim(up_bias[layer], head_index * ff_local, ff_local, 0)
        up_pre = dot(ffn_rows, up_mat, 1, 0) + own_up_bias
        activated = gelu_tanh(up_pre).astype(bf16)
        ffn_out = sum_rows(dot(activated, down_mat, 1, 0))
        kept_values.append(
            (hidden, hidden_mid, normed_rows, own, near, far, context, ffn_rows, up_pre, activated)
        )
        hidden = hidden_mid + (ffn_out + down_bias[layer])

    collected = [None] * LAYERS
    summed = [None] * LAYERS
    for layer in reversed(range(LAYERS)):
        qkv_mat, out_mat, up_mat, down_mat = matrices[layer]
        (layer_input, hidden_mid, normed_rows, own, near, far, context, ffn_rows, up_pre, activated) = (
            kept_values[layer]
        )
        cols = lambda values, i: values[:, i * block : (i + 1) * block]
        grad_low = grad_now.astype(bf16)
        down_bias_grad = jnp.sum(grad_low.astype(f32), axis=0)
        grad_rows = gather_rows(grad_low)
        grad_act = dot(grad_rows, down_mat, 1, 1)
        down_grad = sum_blocks(lambda i: dot(activated, cols(grad_rows, i), 0, 0), 1)
        grad_up = jax.vjp(gelu_tanh, up_pre)[1](grad_act)[0].astype(bf16)
        up_bias_grad = jnp.sum(grad_up.astype(f32), axis=0)
        up_grad = sum_blocks(lambda i: dot(cols(ffn_rows, i), grad_up, 0, 0), 0)
        grad_ffn_normed = sum_rows(dot(grad_up, up_mat, 1, 1))
        ffn_back = jax.vjp(layer_norm, hidden_mid, ffn_gain[layer], ffn_bias[layer])[1]
        grad_mid_part, ffn_gain_grad, ffn_bias_grad = ffn_back(grad_ffn_normed)
        grad_mid = grad_now + grad_mid_part
        attn_low = grad_mid.astype(bf16)
        out_bias_grad = jnp.sum(attn_low.astype(f32), axis=0)
        attn_grad_rows = gather_rows(attn_low)
        grad_context = dot(attn_grad_rows, out_mat, 1, 1).astype(bf16)
        out_grad = sum_blocks(lambda i: dot(context, cols(attn_grad_rows, i), 0, 0), 1)
        own_grad, near_grad, far_grad = attend_back(
            slopes, start_rows, own, near, far, grad_context
        )
        grad_qkv = join_grads(own_grad, to_behind(near_grad, 1), to_behind(far_grad, 2))
        qkv_bias_grad = jnp.sum(grad_qkv.astype(f32), axis=0)
        qkv_grad = sum_blocks(lambda i: dot(cols(normed_rows, i), grad_qkv, 0, 0), 0)
        grad_normed = sum_rows(dot(grad_qkv, qkv_mat, 1, 1))
        attn_back = jax.vjp(layer_norm, layer_input, attn_gain[layer], attn_bias[layer])[1]
        grad_in_part, attn_gain_grad, attn_bias_grad = attn_back(grad_normed)
        grad_now = grad_mid + grad_in_part
        collected[layer] = (qkv_grad, out_grad, up_grad, down_grad)
        common = [
            attn_gain_grad,
            attn_bias_grad,
            out_bias_grad,
            ffn_gain_grad,
            ffn_bias_grad,
            down_bias_grad,
        ]
        if layer == 0:
            emb_back = jax.vjp(layer_norm, embedded_wide, emb_gain, emb_bias)[1]
            embedded_grad, emb_gain_grad, emb_bias_grad = emb_back(grad_now)
            common += [emb_gain_grad, emb_bias_grad]
        common = to_absolute(jnp.stack(common))
        lone = jnp.concatenate([up_bias_grad, qkv_bias_grad])
        count = common.size
        flat = butterfly(jnp.concatenate([common.reshape(-1), lone]), "blk")
        common, lone = flat[:count], flat[count:]
        spread = lax.dynamic_update_slice_in_dim(
            jnp.zeros((lone.size * head_count,), f32), lone, head_index * lone.size, 0
        )
        flat = butterfly(jnp.concatenate([common, spread]), "head")
        common, lone = flat[:count].reshape(-1, D), flat[count:].reshape(head_count, -1)
        bias_sums = lone[:, ff_local:].reshape(H, 3, HD)
        summed[layer] = (
            common,
            lone[:, :ff_local].reshape(-1),
            jnp.stack([bias_sums[:, 0], bias_sums[:, 2]], axis=1),
        )

    def stacked(member):
        return jnp.stack([collected[layer][member] for layer in range(LAYERS)])

    def small(row):
        return jnp.stack([summed[layer][0][row] for layer in range(LAYERS)])

    return (
        to_absolute(hidden),
        to_absolute(embedded_grad),
        summed[0][0][6],
        summed[0][0][7],
        small(0),
        small(1),
        stacked(0),
        jnp.stack([summed[layer][2] for layer in range(LAYERS)]),
        stacked(1),
        small(2),
        small(3),
        small(4),
        stacked(2),
        jnp.stack([summed[layer][1] for layer in range(LAYERS)]),
        stacked(3),
        small(5),
    )


def solution(mesh):
    rows = P(("blk", "head"), None)
    tall, wide = P(None, "blk", "head"), P(None, "head", "blk")
    none = P()
    in_specs = (
        (rows, rows) + (none,) * 5 + (tall, none, wide, none, none, none, tall, none, wide, none)
    )
    out_specs = (
        (rows, rows) + (none,) * 4 + (tall, none, wide, none, none, none, tall, none, wide, none)
    )
    return jax.shard_map(body, mesh=mesh, in_specs=in_specs, out_specs=out_specs, check_vma=False)
```

time: 4790 us -> 1730 us (0.36)
  waiting for transfers between devices: 4000 us -> 999 us
  starting transfers between devices: 122 us -> 220 us
  matrix products: 315 us -> 218 us
  blocking collectives: 96.4 us -> 0 us
  Pallas kernels: 0 us -> 66.3 us
    reduce_scatter x12 -> x8, waiting for transfers between devices: 2300 us -> 62.2 us  [sum_rows(): lax.psum_scatter(values.astype(bf16), 'head', scatter_dimension=0, tiled=...]
    all_gather x12 -> x0, waiting for transfers between devices: 978 us -> none  [the longest x2 305 us: body(): lax.all_gather(qkv_cols, 'head', axis=1, tiled=True)]
    ppermute x28 -> x130, waiting for transfers between devices: 316 us -> 936 us  [the longest x64 441 us: x_swap(): return lax.ppermute(value, 'blk', [(i, i ^ 1) for i in range(8)])]
    psum x2 -> x0, waiting for transfers between devices: 242 us -> none  [body(): lax.psum((emb_gain_grad, emb_bias_grad, stacked(4), stacked(5), stacked(6...]
    ppermute x28 -> x130, starting transfers between devices: 104 us -> 219 us  [the longest x64 109 us: x_swap(): return lax.ppermute(value, 'blk', [(i, i ^ 1) for i in range(8)])]
    dot_general x38 -> x80, matrix products: 315 us -> 218 us  [dot(): lax.dot_general(left, right, (((left_dim,), (right_dim,)), ((), ())), pre...]
    all_to_all x4 -> x0, blocking collectives: 96.4 us -> none  [the longest x2 45.4 us: body(): lax.all_to_all(grad_qkv, 'head', split_axis=0, concat_axis=1, tiled=True)]
    all_gather x4 -> x8, waiting for transfers between devices: 89.7 us -> 0.03 us  [gather_rows(): return lax.all_gather(values, 'head', axis=0, tiled=True)]
  transfers between devices with their start and end apart: 62 -> 146, of which waited for: 53 -> 75; matrix products, arithmetic and copies ran while one was open for 9% -> 18% of each run, Pallas kernels for 0% -> 1%
where the time goes in v1:
time: 1730 us; the launch traced here: 1720 us
  waiting for transfers between devices  999 us (58%)
  starting transfers between devices  220 us (13%)
  matrix products  218 us (13%)
  local copies, waits for them, and re-layouts  109 us (6%)
  other arithmetic  86.2 us (5%)
  Pallas kernels  66.3 us (4%)
    ppermute x64, waiting for transfers between devices, x_swap(): return lax.ppermute(value, 'blk', [(i, i ^ 1) for i in range(8)])  441 us
    ppermute x48, waiting for transfers between devices, z_next(): return lax.ppermute(value, 'blk', pairs)  419 us
    dot_general x80, matrix products, dot(): lax.dot_general(left, right, (((left_dim,), (right_dim,)), ((), ())), pre...  218 us
    ppermute x64, starting transfers between devices, x_swap(): return lax.ppermute(value, 'blk', [(i, i ^ 1) for i in range(8)])  109 us
    unnamed x342, local copies, waits for them, and re-layouts  88.9 us
    ppermute x48, starting transfers between devices, z_next(): return lax.ppermute(value, 'blk', pairs)  77.1 us
    reduce_scatter x8, waiting for transfers between devices, sum_rows(): lax.psum_scatter(values.astype(bf16), 'head', scatter_dimension=0, tiled=...  62.2 us
    ppermute x4, waiting for transfers between devices, to_behind(): lax.ppermute(block, 'blk', [(i + distance, i) for i in range(count - dist...  51.2 us
  transfers between devices with their start and end apart: 146, of which 75 were waited for; matrix products, arithmetic and copies ran while one was open for 18% of the time, Pallas kernels for 1%

profile of v1, /device:TPU:0, one launch (start us, length us, event | category | flops | bytes accessed | tf_op | source)
XLA Modules:
  0.0 1715.6 jit_solution(6909665575802954478)
XLA Ops:
  120.3 21.3 %collective-permute-done.11 = bf16[512,256]{1,0:T(8,128)(2,1)S(1)} collective-permute-done((bf16[512,256]{1,0:T(8,128)(2,1)S(1)}, bf16[512,256]{1,0:T(8,128)(2,1)S(1)}, u32[]{:S(2)}, u32[]{:S(2)}) %collective-permute-start.11) | collective-permute-done | bytes 262176 | tf_op jit(solution)/shard_map/ppermute | solution.py:52
  142.4 16.5 collective-permute-start.15
  197.0 15.1 collective-permute-done.17
  218.3 16.3 collective-permute-done.24
  329.2 20.2 %collective-permute-done.22 = bf16[256,2048]{1,0:T(8,128)(2,1)S(1)} collective-permute-done((bf16[256,2048]{1,0:T(8,128)(2,1)S(1)}, bf16[256,2048]{1,0:T(8,128)(2,1)S(1)}, u32[]{:S(2)}, u32[]{:S(2)}) %collective-permute-start.22) | collective-permute-done | bytes 1048608 | tf_op jit(solution)/shard_map/ppermute | solution.py:52
  350.4 14.9 collective-permute-done.29
  385.4 29.3 %reduce-scatter.11.cloned.1.call-done = bf16[128,2048]{1,0:T(8,128)(2,1)} async-done(((bf16[512,2048]{1,0:T(8,128)(2,1)}), bf16[128,2048]{1,0:T(8,128)(2,1)}) %reduce-scatter.11.cloned.1.call-update) | async-done | bytes 524304 | tf_op jit(solution)/shard_map/reduce_scatter | solution.py:134
  422.6 15.2 collective-permute-done.33
  444.2 19.4 %collective-permute-done.40 = bf16[512,256]{1,0:T(8,128)(2,1)S(1)} collective-permute-done((bf16[512,256]{1,0:T(8,128)(2,1)}, bf16[512,256]{1,0:T(8,128)(2,1)S(1)}, u32[]{:S(2)}, u32[]{:S(2)}) %collective-permute-start.40) | collective-permute-done | bytes 262176 | tf_op jit(solution)/shard_map/ppermute | solution.py:48
  520.0 23.7 %collective-permute-done.41 = bf16[512,256]{1,0:T(8,128)(2,1)S(1)} collective-permute-done((bf16[512,256]{1,0:T(8,128)(2,1)S(1)}, bf16[512,256]{1,0:T(8,128)(2,1)S(1)}, u32[]{:S(2)}, u32[]{:S(2)}) %collective-permute-start.41) | collective-permute-done | bytes 262176 | tf_op jit(solution)/shard_map/ppermute | solution.py:52
  543.8 18.0 %collective-permute-start.45 = (bf16[512,256]{1,0:T(8,128)(2,1)S(1)}, bf16[512,256]{1,0:T(8,128)(2,1)S(1)}, u32[]{:S(2)}, u32[]{:S(2)}) collective-permute-start(bf16[512,256]{1,0:T(8,128)(2,1)S(1)} %collective-permute-done.44), channel_id=1, source_target_pairs={{0,1},{1,0},{2,3},{3,2},{4,5},{5,4},{6,7},{7,6},{8,9},{9,8},{10,11... | collective-permute-start | bytes 786440 | tf_op jit(solution)/shard_map/ppermute | solution.py:52
  584.1 32.8 %reduce-scatter.13.cloned.1.call-done = bf16[128,2048]{1,0:T(8,128)(2,1)} async-done(((bf16[512,2048]{1,0:T(8,128)(2,1)}), bf16[128,2048]{1,0:T(8,128)(2,1)}) %reduce-scatter.13.cloned.1.call-update) | async-done | bytes 524304 | tf_op jit(solution)/shard_map/reduce_scatter | solution.py:134
  625.7 21.8 %collective-permute-done.47 = bf16[256,2048]{1,0:T(8,128)(2,1)} collective-permute-done((bf16[256,2048]{1,0:T(8,128)(2,1)}, bf16[256,2048]{1,0:T(8,128)(2,1)}, u32[]{:S(2)}, u32[]{:S(2)}) %collective-permute-start.47) | collective-permute-done | bytes 1048608 | tf_op jit(solution)/shard_map/ppermute | solution.py:48
  653.3 16.7 collective-permute-done.54
  741.2 17.5 %collective-permute-done.58 = bf16[2048,256]{1,0:T(8,128)(2,1)S(1)} collective-permute-done((bf16[2048,256]{1,0:T(8,128)(2,1)}, bf16[2048,256]{1,0:T(8,128)(2,1)S(1)}, u32[]{:S(2)}, u32[]{:S(2)}) %collective-permute-start.58) | collective-permute-done | bytes 1048608 | tf_op jit(solution)/shard_map/ppermute | solution.py:48
  771.5 20.2 %collective-permute-done.52 = bf16[256,2048]{1,0:T(8,128)(2,1)S(1)} collective-permute-done((bf16[256,2048]{1,0:T(8,128)(2,1)S(1)}, bf16[256,2048]{1,0:T(8,128)(2,1)S(1)}, u32[]{:S(2)}, u32[]{:S(2)}) %collective-permute-start.52) | collective-permute-done | bytes 1048608 | tf_op jit(solution)/shard_map/ppermute | solution.py:52
  792.7 17.7 %collective-permute-done.59 = bf16[2048,256]{1,0:T(8,128)(2,1)S(1)} collective-permute-done((bf16[2048,256]{1,0:T(8,128)(2,1)S(1)}, bf16[2048,256]{1,0:T(8,128)(2,1)S(1)}, u32[]{:S(2)}, u32[]{:S(2)}) %collective-permute-start.59) | collective-permute-done | bytes 1048608 | tf_op jit(solution)/shard_map/ppermute | solution.py:52
  880.3 61.7 %collective-permute-done.112 = bf16[256,2048]{1,0:T(8,128)(2,1)} collective-permute-done((bf16[256,2048]{1,0:T(8,128)(2,1)}, bf16[256,2048]{1,0:T(8,128)(2,1)}, u32[]{:S(2)}, u32[]{:S(2)}) %collective-permute-start.112) | collective-permute-done | bytes 1048608 | tf_op jit(solution)/shard_map/ppermute | solution.py:52
  976.0 18.3 %collective-permute-done.127 = bf16[2048,256]{1,0:T(8,128)(2,1)S(1)} collective-permute-done((bf16[2048,256]{1,0:T(8,128)(2,1)S(1)}, bf16[2048,256]{1,0:T(8,128)(2,1)S(1)}, u32[]{:S(2)}, u32[]{:S(2)}) %collective-permute-start.127) | collective-permute-done | bytes 1048608 | tf_op jit(solution)/shard_map/ppermute | solution.py:48
  1019.9 19.4 %collective-permute-done.128 = bf16[2048,256]{1,0:T(8,128)(2,1)} collective-permute-done((bf16[2048,256]{1,0:T(8,128)(2,1)}, bf16[2048,256]{1,0:T(8,128)(2,1)}, u32[]{:S(2)}, u32[]{:S(2)}) %collective-permute-start.128) | collective-permute-done | bytes 1048608 | tf_op jit(solution)/shard_map/ppermute | solution.py:48
  1051.5 16.8 attend_back.2
  1090.7 22.7 %collective-permute-done.61.far_ref = bf16[512,1024]{1,0:T(8,128)(2,1)} collective-permute-done((bf16[512,1024]{1,0:T(8,128)(2,1)}, bf16[512,1024]{1,0:T(8,128)(2,1)}, u32[]{:S(2)}, u32[]{:S(2)}) %collective-permute-start.61) | collective-permute-done | bytes 1048608 | tf_op jit(solution)/shard_map/ppermute | solution.py:126
  1157.5 28.4 %collective-permute-done.84 = bf16[256,1536]{1,0:T(8,128)(2,1)S(1)} collective-permute-done((bf16[256,1536]{1,0:T(8,128)(2,1)S(1)}, bf16[256,1536]{1,0:T(8,128)(2,1)S(1)}, u32[]{:S(2)}, u32[]{:S(2)}) %collective-permute-start.84) | collective-permute-done | bytes 786464 | tf_op jit(solution)/shard_map/ppermute | solution.py:52
  1232.5 20.6 %collective-permute-done.87 = bf16[256,1536]{1,0:T(8,128)(2,1)S(1)} collective-permute-done((bf16[256,1536]{1,0:T(8,128)(2,1)S(1)}, bf16[256,1536]{1,0:T(8,128)(2,1)S(1)}, u32[]{:S(2)}, u32[]{:S(2)}) %collective-permute-start.87) | collective-permute-done | bytes 786464 | tf_op jit(solution)/shard_map/ppermute | solution.py:48
  1292.0 82.1 %collective-permute-done.105 = bf16[256,2048]{1,0:T(8,128)(2,1)S(1)} collective-permute-done((bf16[256,2048]{1,0:T(8,128)(2,1)S(1)}, bf16[256,2048]{1,0:T(8,128)(2,1)S(1)}, u32[]{:S(2)}, u32[]{:S(2)}) %collective-permute-start.105) | collective-permute-done | bytes 1048608 | tf_op jit(solution)/shard_map/ppermute | solution.py:52
  1404.9 20.3 %collective-permute-done.120 = bf16[2048,256]{1,0:T(8,128)(2,1)S(1)} collective-permute-done((bf16[2048,256]{1,0:T(8,128)(2,1)S(1)}, bf16[2048,256]{1,0:T(8,128)(2,1)S(1)}, u32[]{:S(2)}, u32[]{:S(2)}) %collective-permute-start.120) | collective-permute-done | bytes 1048608 | tf_op jit(solution)/shard_map/ppermute | solution.py:48
  1449.9 20.3 %collective-permute-done.121 = bf16[2048,256]{1,0:T(8,128)(2,1)} collective-permute-done((bf16[2048,256]{1,0:T(8,128)(2,1)}, bf16[2048,256]{1,0:T(8,128)(2,1)}, u32[]{:S(2)}, u32[]{:S(2)}) %collective-permute-start.121) | collective-permute-done | bytes 1048608 | tf_op jit(solution)/shard_map/ppermute | solution.py:48
  1475.9 16.7 collective-permute-done.108
  1494.4 17.8 %collective-permute-done.122 = bf16[2048,256]{1,0:T(8,128)(2,1)S(1)} collective-permute-done((bf16[2048,256]{1,0:T(8,128)(2,1)S(1)}, bf16[2048,256]{1,0:T(8,128)(2,1)S(1)}, u32[]{:S(2)}, u32[]{:S(2)}) %collective-permute-start.122) | collective-permute-done | bytes 1048608 | tf_op jit(solution)/shard_map/ppermute | solution.py:48
  1518.7 16.9 attend_back.3
  1548.2 20.1 %collective-permute-done.91 = bf16[512,256]{1,0:T(8,128)(2,1)S(1)} collective-permute-done((bf16[512,256]{1,0:T(8,128)(2,1)S(1)}, bf16[512,256]{1,0:T(8,128)(2,1)S(1)}, u32[]{:S(2)}, u32[]{:S(2)}) %collective-permute-start.91) | collective-permute-done | bytes 262176 | tf_op jit(solution)/shard_map/ppermute | solution.py:52
  1570.5 16.4 collective-permute-done.63.far_ref
  (871 shorter events, 963.4 us)
Async XLA Ops:
  7.3 91.0 %all-gather.9.cloned.1.call-start = ((), (), s32[]{:S(2)}) async-start(), calls=%async_computation.8 | async-start | bytes 2621440 | tf_op jit(solution)/shard_map/all_gather | solution.py:130
  14.2 101.6 %collective-permute-start.9 = (bf16[512,256]{1,0:T(8,128)(2,1)}, bf16[512,256]{1,0:T(8,128)(2,1)}, u32[]{:S(2)}, u32[]{:S(2)}) collective-permute-start(bf16[512,256]{1,0:T(8,128)(2,1)} %get-tuple-element.93), channel_id=1, source_target_pairs={{0,1},{1,0},{2,3},{3,2},{4,5},{5,4},{6,7},{7,6},{8,9},{9,8},{10,11... | collective-permute-start | bytes 786440 | tf_op jit(solution)/shard_map/ppermute | solution.py:52
  25.1 218.0 %reduce-scatter.9.cloned.1.call-start = ((), (), s32[]{:S(2)}) async-start(), calls=%async_computation.9 | async-start | bytes 2621440 | tf_op jit(solution)/shard_map/reduce_scatter | solution.py:134
  180.7 185.6 %all-gather.11.cloned.1.call-start = ((), (), s32[]{:S(2)}) async-start(), calls=%async_computation.10 | async-start | bytes 2621440 | tf_op jit(solution)/shard_map/all_gather | solution.py:130
  247.7 167.0 %reduce-scatter.11.cloned.1.call-start = ((), (), s32[]{:S(2)}) async-start(), calls=%async_computation.11 | async-start | bytes 2621440 | tf_op jit(solution)/shard_map/reduce_scatter | solution.py:134
  385.0 118.0 %all-gather.13.cloned.1.call-start = ((), (), s32[]{:S(2)}) async-start(), calls=%async_computation.12 | async-start | bytes 2621440 | tf_op jit(solution)/shard_map/all_gather | solution.py:130
  417.7 199.2 %reduce-scatter.13.cloned.1.call-start = ((), (), s32[]{:S(2)}) async-start(), calls=%async_computation.13 | async-start | bytes 2621440 | tf_op jit(solution)/shard_map/reduce_scatter | solution.py:134
  443.6 73.4 %collective-permute-start.39 = (bf16[512,256]{1,0:T(8,128)(2,1)}, bf16[512,256]{1,0:T(8,128)(2,1)}, u32[]{:S(2)}, u32[]{:S(2)}) collective-permute-start(bf16[512,256]{1,0:T(8,128)(2,1)} %get-tuple-element.92), channel_id=1, source_target_pairs={{0,1},{1,0},{2,3},{3,2},{4,5},{5,4},{6,7},{7,6},{8,9},{9,8},{10,11... | collective-permute-start | bytes 786440 | tf_op jit(solution)/shard_map/ppermute | solution.py:52
  584.1 227.5 %all-gather.15.cloned.1.call-start = ((), (), s32[]{:S(2)}) async-start(), calls=%async_computation.14 | async-start | bytes 2621440 | tf_op jit(solution)/shard_map/all_gather | solution.py:130
  620.3 201.8 %all-gather.17.cloned.1.call-start = ((), (), s32[]{:S(2)}) async-start(), calls=%async_computation.16 | async-start | bytes 2621440 | tf_op jit(solution)/shard_map/all_gather | solution.py:130
  675.4 321.4 %reduce-scatter.17.cloned.1.call-start = ((), (), s32[]{:S(2)}) async-start(), calls=%async_computation.17 | async-start | bytes 2621440 | tf_op jit(solution)/shard_map/reduce_scatter | solution.py:134
  844.4 154.3 %reduce-scatter.15.cloned.1.call-start = ((), (), s32[]{:S(2)}) async-start(), calls=%async_computation.15 | async-start | bytes 2621440 | tf_op jit(solution)/shard_map/reduce_scatter | solution.py:134
  848.2 290.1 %collective-permute-start.123 = (bf16[2048,256]{1,0:T(8,128)(2,1)}, bf16[2048,256]{1,0:T(8,128)(2,1)}, u32[]{:S(2)}, u32[]{:S(2)}) collective-permute-start(bf16[2048,256]{1,0:T(8,128)(2,1)} %convolution_convert_fusion.11), channel_id=1, source_target_pairs={{0,1},{1,0},{2,3},{3,2},{4,5},{5,4},{6,7},{7,6},{8,9},{9,8},{10,11... | collective-permute-start | bytes 3145736 | tf_op jit(solution)/shard_map/ppermute | solution.py:52
  852.5 123.5 %collective-permute-start.125 = (bf16[2048,256]{1,0:T(8,128)(2,1)}, bf16[2048,256]{1,0:T(8,128)(2,1)}, u32[]{:S(2)}, u32[]{:S(2)}) collective-permute-start(bf16[2048,256]{1,0:T(8,128)(2,1)} %convolution_convert_fusion.9), channel_id=1, source_target_pairs={{0,1},{1,0},{2,3},{3,2},{4,5},{5,4},{6,7},{7,6},{8,9},{9,8},{10,11... | collective-permute-start | bytes 3145736 | tf_op jit(solution)/shard_map/ppermute | solution.py:52
  856.1 89.7 %collective-permute-start.126 = (bf16[2048,256]{1,0:T(8,128)(2,1)}, bf16[2048,256]{1,0:T(8,128)(2,1)}, u32[]{:S(2)}, u32[]{:S(2)}) collective-permute-start(bf16[2048,256]{1,0:T(8,128)(2,1)} %convolution_convert_fusion.8), channel_id=1, source_target_pairs={{0,1},{1,0},{2,3},{3,2},{4,5},{5,4},{6,7},{7,6},{8,9},{9,8},{10,11... | collective-permute-start | bytes 3145736 | tf_op jit(solution)/shard_map/ppermute | solution.py:52
  859.9 82.0 %collective-permute-start.112 = (bf16[256,2048]{1,0:T(8,128)(2,1)}, bf16[256,2048]{1,0:T(8,128)(2,1)}, u32[]{:S(2)}, u32[]{:S(2)}) collective-permute-start(bf16[256,2048]{1,0:T(8,128)(2,1)} %convolution_convert_fusion.16), channel_id=1, source_target_pairs={{0,1},{1,0},{2,3},{3,2},{4,5},{5,4},{6,7},{7,6},{8,9},{9,8},{10,11... | collective-permute-start | bytes 3145736 | tf_op jit(solution)/shard_map/ppermute | solution.py:52
  863.4 98.0 %collective-permute-start.111 = (bf16[256,2048]{1,0:T(8,128)(2,1)}, bf16[256,2048]{1,0:T(8,128)(2,1)}, u32[]{:S(2)}, u32[]{:S(2)}) collective-permute-start(bf16[256,2048]{1,0:T(8,128)(2,1)} %convolution_convert_fusion.17), channel_id=1, source_target_pairs={{0,1},{1,0},{2,3},{3,2},{4,5},{5,4},{6,7},{7,6},{8,9},{9,8},{10,11... | collective-permute-start | bytes 3145736 | tf_op jit(solution)/shard_map/ppermute | solution.py:52
  870.4 176.8 %all-gather.19.cloned.1.call-start = ((), (), s32[]{:S(2)}) async-start(), calls=%async_computation.18 | async-start | bytes 2621440 | tf_op jit(solution)/shard_map/all_gather | solution.py:130
  1003.8 183.6 %reduce-scatter.19.cloned.1.call-start = ((), (), s32[]{:S(2)}) async-start(), calls=%async_computation.19 | async-start | bytes 2621440 | tf_op jit(solution)/shard_map/reduce_scatter | solution.py:134
  1007.2 122.4 %collective-permute-start.109 = (bf16[256,2048]{1,0:T(8,128)(2,1)}, bf16[256,2048]{1,0:T(8,128)(2,1)}, u32[]{:S(2)}, u32[]{:S(2)}) collective-permute-start(bf16[256,2048]{1,0:T(8,128)(2,1)} %convolution_convert_fusion.19), channel_id=1, source_target_pairs={{0,1},{1,0},{2,3},{3,2},{4,5},{5,4},{6,7},{7,6},{8,9},{9,8},{10,11... | collective-permute-start | bytes 3145736 | tf_op jit(solution)/shard_map/ppermute | solution.py:52
  1019.9 111.0 %collective-permute-start.115 = (bf16[256,2048]{1,0:T(8,128)(2,1)}, bf16[256,2048]{1,0:T(8,128)(2,1)}, u32[]{:S(2)}, u32[]{:S(2)}) collective-permute-start(bf16[256,2048]{1,0:T(8,128)(2,1)} %add_convert_fusion.6), channel_id=1, source_target_pairs={{0,2},{1,3},{2,4},{3,5},{4,6},{5,7},{6,0},{7,1},{8,10},{9,11},{10,... | collective-permute-start | bytes 3145736 | tf_op jit(solution)/shard_map/ppermute | solution.py:48
  1126.0 130.0 %all-gather.21.cloned.1.call-start = ((), (), s32[]{:S(2)}) async-start(), calls=%async_computation.20 | async-start | bytes 2621440 | tf_op jit(solution)/shard_map/all_gather | solution.py:130
  1148.4 84.0 %collective-permute-start.81 = (bf16[256,1536]{1,0:T(8,128)(2,1)}, bf16[256,1536]{1,0:T(8,128)(2,1)S(1)}, u32[]{:S(2)}, u32[]{:S(2)}) collective-permute-start(bf16[256,1536]{1,0:T(8,128)(2,1)} %convolution_convert_fusion.27), channel_id=1, source_target_pairs={{0,1},{1,0},{2,3},{3,2},{4,5},{5,4},{6,7},{7,6},{8,9},{9,8},{10,11... | collective-permute-start | bytes 2359304 | tf_op jit(solution)/shard_map/ppermute | solution.py:52
  1152.6 75.5 %collective-permute-start.82 = (bf16[256,1536]{1,0:T(8,128)(2,1)}, bf16[256,1536]{1,0:T(8,128)(2,1)}, u32[]{:S(2)}, u32[]{:S(2)}) collective-permute-start(bf16[256,1536]{1,0:T(8,128)(2,1)} %convolution_convert_fusion.26), channel_id=1, source_target_pairs={{0,1},{1,0},{2,3},{3,2},{4,5},{5,4},{6,7},{7,6},{8,9},{9,8},{10,11... | collective-permute-start | bytes 2359304 | tf_op jit(solution)/shard_map/ppermute | solution.py:52
  1227.2 199.6 %reduce-scatter.21.cloned.1.call-start = ((), (), s32[]{:S(2)}) async-start(), calls=%async_computation.21 | async-start | bytes 2621440 | tf_op jit(solution)/shard_map/reduce_scatter | solution.py:134
  1276.5 238.5 %all-gather.23.cloned.1.call-start = ((), (), s32[]{:S(2)}) async-start(), calls=%async_computation.22 | async-start | bytes 2621440 | tf_op jit(solution)/shard_map/all_gather | solution.py:130
  1280.4 213.9 %collective-permute-start.116 = (bf16[2048,256]{1,0:T(8,128)(2,1)}, bf16[2048,256]{1,0:T(8,128)(2,1)}, u32[]{:S(2)}, u32[]{:S(2)}) collective-permute-start(bf16[2048,256]{1,0:T(8,128)(2,1)} %convolution_convert_fusion.15), channel_id=1, source_target_pairs={{0,1},{1,0},{2,3},{3,2},{4,5},{5,4},{6,7},{7,6},{8,9},{9,8},{10,11... | collective-permute-start | bytes 3145736 | tf_op jit(solution)/shard_map/ppermute | solution.py:52
  1281.8 123.0 %collective-permute-start.118 = (bf16[2048,256]{1,0:T(8,128)(2,1)S(1)}, bf16[2048,256]{1,0:T(8,128)(2,1)S(1)}, u32[]{:S(2)}, u32[]{:S(2)}) collective-permute-start(bf16[2048,256]{1,0:T(8,128)(2,1)S(1)} %convolution_convert_fusion.13), channel_id=1, source_target_pairs={{0,1},{1,0},{2,3},{3,2},{4,5},{5,4},{6,7},{7,6},{8,9},{9,8},{10,11... | collective-permute-start | bytes 3145736 | tf_op jit(solution)/shard_map/ppermute | solution.py:52
  1284.1 92.5 %collective-permute-start.119 = (bf16[2048,256]{1,0:T(8,128)(2,1)S(1)}, bf16[2048,256]{1,0:T(8,128)(2,1)S(1)}, u32[]{:S(2)}, u32[]{:S(2)}) collective-permute-start(bf16[2048,256]{1,0:T(8,128)(2,1)S(1)} %convolution_convert_fusion.12), channel_id=1, source_target_pairs={{0,1},{1,0},{2,3},{3,2},{4,5},{5,4},{6,7},{7,6},{8,9},{9,8},{10,11... | collective-permute-start | bytes 3145736 | tf_op jit(solution)/shard_map/ppermute | solution.py:52
  1285.5 88.6 %collective-permute-start.105 = (bf16[256,2048]{1,0:T(8,128)(2,1)S(1)}, bf16[256,2048]{1,0:T(8,128)(2,1)S(1)}, u32[]{:S(2)}, u32[]{:S(2)}) collective-permute-start(bf16[256,2048]{1,0:T(8,128)(2,1)S(1)} %convolution_convert_fusion.20), channel_id=1, source_target_pairs={{0,1},{1,0},{2,3},{3,2},{4,5},{5,4},{6,7},{7,6},{8,9},{9,8},{10,11... | collective-permute-start | bytes 3145736 | tf_op jit(solution)/shard_map/ppermute | solution.py:52
  1287.8 107.8 %collective-permute-start.104 = (bf16[256,2048]{1,0:T(8,128)(2,1)S(1)}, bf16[256,2048]{1,0:T(8,128)(2,1)S(1)}, u32[]{:S(2)}, u32[]{:S(2)}) collective-permute-start(bf16[256,2048]{1,0:T(8,128)(2,1)S(1)} %convolution_convert_fusion.21), channel_id=1, source_target_pairs={{0,1},{1,0},{2,3},{3,2},{4,5},{5,4},{6,7},{7,6},{8,9},{9,8},{10,11... | collective-permute-start | bytes 3145736 | tf_op jit(solution)/shard_map/ppermute | solution.py:52
  1432.7 241.0 %reduce-scatter.23.cloned.1.call-start = ((), (), s32[]{:S(2)}) async-start(), calls=%async_computation.23 | async-start | bytes 2621440 | tf_op jit(solution)/shard_map/reduce_scatter | solution.py:134
  (232 other events, 9576.9 us)
Sparse Core Ops, SparseCore 0:
  25.2 21.7 all-gather.8
  180.9 33.5 reduce-scatter.8
  247.9 19.8 all-gather.10
  385.1 29.5 reduce-scatter.10
  417.8 22.5 all-gather.12
  584.2 32.6 reduce-scatter.12
  620.4 22.5 all-gather.14
  675.6 19.7 all-gather.16
  844.6 28.3 reduce-scatter.16
  875.3 31.1 reduce-scatter.14
  1003.9 23.0 all-gather.18
  1126.1 30.4 reduce-scatter.18
  1227.3 22.6 all-gather.20
  1276.6 28.6 reduce-scatter.20
  1432.8 22.1 all-gather.22
  1601.1 28.8 reduce-scatter.22

commit v2 on v1

--- a/solution.py
+++ b/solution.py
@@ -1,11 +1,10 @@
-from functools import partial
-
 import jax
 import jax.numpy as jnp
 from jax import lax
 from jax.experimental import pallas as pl
 from jax.experimental.pallas import tpu as pltpu
 from jax.sharding import PartitionSpec as P
+
 
 D = 2048
 H = 16
@@ -78,28 +77,39 @@
     return jnp.where(x == 0, turned, jnp.concatenate(swapped, -1))
 
 
-def gather_blocks(shard, axis):
+BALANCED = ("q", "u")
+
+
+def gather_blocks(shard, axis, tag):
     if not ring_ok():
         return lax.all_gather(shard, "blk", axis=axis, tiled=True)
     held = [shard]
-    for _ in range(3):
+    for _ in range(1, 4):
         held.append(z_next(held[-1], -1))
-    pieces = []
-    for piece in held:
-        pieces += [piece, x_swap(piece)]
-    return jnp.concatenate(pieces, axis)
-
-
-def sum_blocks(piece_of, axis):
+    across = [x_swap(held[k]) for k in range(3)]
+    if tag[-1] in BALANCED:
+        across.append(z_next(across[0], 1))
+    else:
+        across.append(x_swap(held[3]))
+    return jnp.concatenate([p for pair in zip(held, across) for p in pair], axis)
+
+
+def sum_blocks(piece_of, axis, tag):
     if not ring_ok():
         whole = jnp.concatenate([piece_of(i) for i in range(lax.axis_size("blk"))], axis)
         return lax.psum_scatter(
             whole.astype(bf16), "blk", scatter_dimension=axis, tiled=True
         ).astype(f32)
-    total = None
+    balanced = tag[-1] in BALANCED
+    total = aside = None
     for k in (3, 2, 1, 0):
-        came = x_swap(piece_of(2 * k + 1).astype(bf16))
-        mine = piece_of(2 * k).astype(f32) + came.astype(f32)
+        mine, other = piece_of(2 * k), piece_of(2 * k + 1)
+        if balanced and k == 3:
+            aside = z_next(other.astype(bf16), -1)
+        else:
+            if balanced and k == 0:
+                other = other + aside.astype(f32)
+            mine = mine + x_swap(other.astype(bf16)).astype(f32)
         if total is not None:
             mine = mine + total.astype(f32)
         if k > 0:
@@ -268,7 +278,7 @@
     )(own, near, far)
 
 
-def body(
+def program(
     embedded,
     cotangent,
     doc_lengths,
@@ -309,10 +319,10 @@
     for layer in range(LAYERS):
         matrices.append(
             (
-                gather_blocks(qkv_weight[layer], 0),
-                gather_blocks(out_weight[layer], 1),
-                gather_blocks(up_weight[layer], 0),
-                gather_blocks(down_weight[layer], 1),
+                gather_blocks(qkv_weight[layer], 0, f"{layer}q"),
+                gather_blocks(out_weight[layer], 1, f"{layer}o"),
+                gather_blocks(up_weight[layer], 0, f"{layer}u"),
+                gather_blocks(down_weight[layer], 1, f"{layer}d"),
             )
         )
 
@@ -371,10 +381,10 @@
         down_bias_grad = jnp.sum(grad_low.astype(f32), axis=0)
         grad_rows = gather_rows(grad_low)
         grad_act = dot(grad_rows, down_mat, 1, 1)
-        down_grad = sum_blocks(lambda i: dot(activated, cols(grad_rows, i), 0, 0), 1)
+        down_grad = sum_blocks(lambda i: dot(activated, cols(grad_rows, i), 0, 0), 1, f"{layer}d")
         grad_up = jax.vjp(gelu_tanh, up_pre)[1](grad_act)[0].astype(bf16)
         up_bias_grad = jnp.sum(grad_up.astype(f32), axis=0)
-        up_grad = sum_blocks(lambda i: dot(cols(ffn_rows, i), grad_up, 0, 0), 0)
+        up_grad = sum_blocks(lambda i: dot(cols(ffn_rows, i), grad_up, 0, 0), 0, f"{layer}u")
         grad_ffn_normed = sum_rows(dot(grad_up, up_mat, 1, 1))
         ffn_back = jax.vjp(layer_norm, hidden_mid, ffn_gain[layer], ffn_bias[layer])[1]
         grad_mid_part, ffn_gain_grad, ffn_bias_grad = ffn_back(grad_ffn_normed)
@@ -383,13 +393,13 @@
         out_bias_grad = jnp.sum(attn_low.astype(f32), axis=0)
         attn_grad_rows = gather_rows(attn_low)
         grad_context = dot(attn_grad_rows, out_mat, 1, 1).astype(bf16)
-        out_grad = sum_blocks(lambda i: dot(context, cols(attn_grad_rows, i), 0, 0), 1)
+        out_grad = sum_blocks(lambda i: dot(context, cols(attn_grad_rows, i), 0, 0), 1, f"{layer}o")
         own_grad, near_grad, far_grad = attend_back(
             slopes, start_rows, own, near, far, grad_context
         )
         grad_qkv = join_grads(own_grad, to_behind(near_grad, 1), to_behind(far_grad, 2))
         qkv_bias_grad = jnp.sum(grad_qkv.astype(f32), axis=0)
-        qkv_grad = sum_blocks(lambda i: dot(cols(normed_rows, i), grad_qkv, 0, 0), 0)
+        qkv_grad = sum_blocks(lambda i: dot(cols(normed_rows, i), grad_qkv, 0, 0), 0, f"{layer}q")
         grad_normed = sum_rows(dot(grad_qkv, qkv_mat, 1, 1))
         attn_back = jax.vjp(layer_norm, layer_input, attn_gain[layer], attn_bias[layer])[1]
         grad_in_part, attn_gain_grad, attn_bias_grad = attn_back(grad_normed)
@@ -460,4 +470,4 @@
     out_specs = (
         (rows, rows) + (none,) * 4 + (tall, none, wide, none, none, none, tall, none, wide, none)
     )
-    return jax.shard_map(body, mesh=mesh, in_specs=in_specs, out_specs=out_specs, check_vma=False)
+    return jax.shard_map(program, mesh=mesh, in_specs=in_specs, out_specs=out_specs, check_vma=False)

time: 1730 us -> 1580 us (0.913)
  waiting for transfers between devices: 999 us -> 853 us
    ppermute x64 -> x56, waiting for transfers between devices: 441 us -> 310 us  [x_swap(): return lax.ppermute(value, 'blk', [(i, i ^ 1) for i in range(8)])]
    ppermute x48 -> x56, starting transfers between devices: 77.1 us -> 99 us  [z_next(): return lax.ppermute(value, 'blk', pairs)]
    ppermute x48 -> x56, waiting for transfers between devices: 419 us -> 405 us  [z_next(): return lax.ppermute(value, 'blk', pairs)]
    ppermute x64 -> x56, starting transfers between devices: 109 us -> 96.1 us  [x_swap(): return lax.ppermute(value, 'blk', [(i, i ^ 1) for i in range(8)])]
    unnamed x342 -> x344, local copies, waits for them, and re-layouts: 88.9 us -> 88.1 us
  transfers between devices with their start and end apart: 146 -> 146, of which waited for: 75 -> 73; matrix products, arithmetic and copies ran while one was open for 18% -> 20% of each run, Pallas kernels for 1% -> 3%
where the time goes in v2:
time: 1580 us; the launch traced here: 1570 us
  waiting for transfers between devices  853 us (54%)
  starting transfers between devices  225 us (14%)
  matrix products  219 us (14%)
  local copies, waits for them, and re-layouts  108 us (7%)
  other arithmetic  77.1 us (5%)
  Pallas kernels  66.1 us (4%)
  between operations  17 us (1%)
    ppermute x56, waiting for transfers between devices, z_next(): return lax.ppermute(value, 'blk', pairs)  405 us
    ppermute x56, waiting for transfers between devices, x_swap(): return lax.ppermute(value, 'blk', [(i, i ^ 1) for i in range(8)])  310 us
    dot_general x80, matrix products, dot(): lax.dot_general(left, right, (((left_dim,), (right_dim,)), ((), ())), pre...  219 us
    ppermute x56, starting transfers between devices, z_next(): return lax.ppermute(value, 'blk', pairs)  99 us
    ppermute x56, starting transfers between devices, x_swap(): return lax.ppermute(value, 'blk', [(i, i ^ 1) for i in range(8)])  96.1 us
    unnamed x344, local copies, waits for them, and re-layouts  88.1 us
    reduce_scatter x8, waiting for transfers between devices, sum_rows(): lax.psum_scatter(values.astype(bf16), 'head', scatter_dimension=0, tiled=...  60.6 us
    ppermute x4, waiting for transfers between devices, to_behind(): lax.ppermute(block, 'blk', [(i + distance, i) for i in range(count - dist...  43.2 us
  transfers between devices with their start and end apart: 146, of which 73 were waited for; matrix products, arithmetic and copies ran while one was open for 20% of the time, Pallas kernels for 3%

profile of v2, /device:TPU:0, one launch (start us, length us, event | category | flops | bytes accessed | tf_op | source)
XLA Modules:
  0.0 1565.6 jit_solution(17262816571828245109)
XLA Ops:
  45.1 14.4 collective-permute-done.3
  120.6 23.1 %collective-permute-done.11 = bf16[512,256]{1,0:T(8,128)(2,1)S(1)} collective-permute-done((bf16[512,256]{1,0:T(8,128)(2,1)S(1)}, bf16[512,256]{1,0:T(8,128)(2,1)S(1)}, u32[]{:S(2)}, u32[]{:S(2)}) %collective-permute-start.11) | collective-permute-done | bytes 262176 | tf_op jit(solution)/shard_map/ppermute | solution.py:51
  144.5 17.0 %collective-permute-start.15 = (bf16[512,256]{1,0:T(8,128)(2,1)S(1)}, bf16[512,256]{1,0:T(8,128)(2,1)S(1)}, u32[]{:S(2)}, u32[]{:S(2)}) collective-permute-start(bf16[512,256]{1,0:T(8,128)(2,1)S(1)} %collective-permute-done.14), channel_id=1, source_target_pairs={{0,1},{1,0},{2,3},{3,2},{4,5},{5,4},{6,7},{7,6},{8,9},{9,8},{10,11... | collective-permute-start | bytes 786440 | tf_op jit(solution)/shard_map/ppermute | solution.py:51
  200.7 15.2 collective-permute-done.17
  221.1 17.3 %collective-permute-done.24 = bf16[2048,256]{1,0:T(8,128)(2,1)} collective-permute-done((bf16[2048,256]{1,0:T(8,128)(2,1)}, bf16[2048,256]{1,0:T(8,128)(2,1)}, u32[]{:S(2)}, u32[]{:S(2)}) %collective-permute-start.24) | collective-permute-done | bytes 1048608 | tf_op jit(solution)/shard_map/ppermute | solution.py:47
  254.0 26.7 %collective-permute-done.26 = bf16[2048,256]{1,0:T(8,128)(2,1)} collective-permute-done((bf16[2048,256]{1,0:T(8,128)(2,1)}, bf16[2048,256]{1,0:T(8,128)(2,1)}, u32[]{:S(2)}, u32[]{:S(2)}) %collective-permute-start.26) | collective-permute-done | bytes 1048608 | tf_op jit(solution)/shard_map/ppermute | solution.py:47
  301.4 25.8 %collective-permute-done.28 = bf16[2048,256]{1,0:T(8,128)(2,1)S(1)} collective-permute-done((bf16[2048,256]{1,0:T(8,128)(2,1)}, bf16[2048,256]{1,0:T(8,128)(2,1)S(1)}, u32[]{:S(2)}, u32[]{:S(2)}) %collective-permute-start.28) | collective-permute-done | bytes 1048608 | tf_op jit(solution)/shard_map/ppermute | solution.py:47
  334.8 15.6 collective-permute-done.21
  376.6 27.9 %reduce-scatter.11.cloned.1.call-done = bf16[128,2048]{1,0:T(8,128)(2,1)} async-done(((bf16[512,2048]{1,0:T(8,128)(2,1)}), bf16[128,2048]{1,0:T(8,128)(2,1)}) %reduce-scatter.11.cloned.1.call-update) | async-done | bytes 524304 | tf_op jit(solution)/shard_map/reduce_scatter | solution.py:144
  415.2 18.2 %collective-permute-done.40 = bf16[512,256]{1,0:T(8,128)(2,1)S(1)} collective-permute-done((bf16[512,256]{1,0:T(8,128)(2,1)}, bf16[512,256]{1,0:T(8,128)(2,1)S(1)}, u32[]{:S(2)}, u32[]{:S(2)}) %collective-permute-start.40) | collective-permute-done | bytes 262176 | tf_op jit(solution)/shard_map/ppermute | solution.py:47
  453.0 16.4 %collective-permute-done.34 = bf16[256,1536]{1,0:T(8,128)(2,1)S(1)} collective-permute-done((bf16[256,1536]{1,0:T(8,128)(2,1)}, bf16[256,1536]{1,0:T(8,128)(2,1)S(1)}, u32[]{:S(2)}, u32[]{:S(2)}) %collective-permute-start.34) | collective-permute-done | bytes 786464 | tf_op jit(solution)/shard_map/ppermute | solution.py:51
  497.0 24.9 %collective-permute-done.41 = bf16[512,256]{1,0:T(8,128)(2,1)S(1)} collective-permute-done((bf16[512,256]{1,0:T(8,128)(2,1)S(1)}, bf16[512,256]{1,0:T(8,128)(2,1)S(1)}, u32[]{:S(2)}, u32[]{:S(2)}) %collective-permute-start.41) | collective-permute-done | bytes 262176 | tf_op jit(solution)/shard_map/ppermute | solution.py:51
  522.0 18.5 %collective-permute-start.45 = (bf16[512,256]{1,0:T(8,128)(2,1)S(1)}, bf16[512,256]{1,0:T(8,128)(2,1)S(1)}, u32[]{:S(2)}, u32[]{:S(2)}) collective-permute-start(bf16[512,256]{1,0:T(8,128)(2,1)S(1)} %collective-permute-done.44), channel_id=1, source_target_pairs={{0,1},{1,0},{2,3},{3,2},{4,5},{5,4},{6,7},{7,6},{8,9},{9,8},{10,11... | collective-permute-start | bytes 786440 | tf_op jit(solution)/shard_map/ppermute | solution.py:51
  563.1 32.6 %reduce-scatter.13.cloned.1.call-done = bf16[128,2048]{1,0:T(8,128)(2,1)} async-done(((bf16[512,2048]{1,0:T(8,128)(2,1)}), bf16[128,2048]{1,0:T(8,128)(2,1)}) %reduce-scatter.13.cloned.1.call-update) | async-done | bytes 524304 | tf_op jit(solution)/shard_map/reduce_scatter | solution.py:144
  605.0 21.3 %collective-permute-done.54 = bf16[2048,256]{1,0:T(8,128)(2,1)} collective-permute-done((bf16[2048,256]{1,0:T(8,128)(2,1)}, bf16[2048,256]{1,0:T(8,128)(2,1)}, u32[]{:S(2)}, u32[]{:S(2)}) %collective-permute-start.54) | collective-permute-done | bytes 1048608 | tf_op jit(solution)/shard_map/ppermute | solution.py:47
  631.7 17.1 %collective-permute-done.47 = bf16[256,2048]{1,0:T(8,128)(2,1)} collective-permute-done((bf16[256,2048]{1,0:T(8,128)(2,1)}, bf16[256,2048]{1,0:T(8,128)(2,1)}, u32[]{:S(2)}, u32[]{:S(2)}) %collective-permute-start.47) | collective-permute-done | bytes 1048608 | tf_op jit(solution)/shard_map/ppermute | solution.py:47
  679.4 14.4 collective-permute-done.49
  726.5 20.2 %collective-permute-done.50 = bf16[256,2048]{1,0:T(8,128)(2,1)S(1)} collective-permute-done((bf16[256,2048]{1,0:T(8,128)(2,1)S(1)}, bf16[256,2048]{1,0:T(8,128)(2,1)S(1)}, u32[]{:S(2)}, u32[]{:S(2)}) %collective-permute-start.50) | collective-permute-done | bytes 1048608 | tf_op jit(solution)/shard_map/ppermute | solution.py:51
  840.4 34.1 %collective-permute-done.112 = bf16[256,2048]{1,0:T(8,128)(2,1)} collective-permute-done((bf16[256,2048]{1,0:T(8,128)(2,1)}, bf16[256,2048]{1,0:T(8,128)(2,1)}, u32[]{:S(2)}, u32[]{:S(2)}) %collective-permute-start.112) | collective-permute-done | bytes 1048608 | tf_op jit(solution)/shard_map/ppermute | solution.py:51
  907.7 19.5 %collective-permute-done.127 = bf16[2048,256]{1,0:T(8,128)(2,1)S(1)} collective-permute-done((bf16[2048,256]{1,0:T(8,128)(2,1)S(1)}, bf16[2048,256]{1,0:T(8,128)(2,1)S(1)}, u32[]{:S(2)}, u32[]{:S(2)}) %collective-permute-start.127) | collective-permute-done | bytes 1048608 | tf_op jit(solution)/shard_map/ppermute | solution.py:47
  941.9 22.5 %collective-permute-done.128 = bf16[2048,256]{1,0:T(8,128)(2,1)} collective-permute-done((bf16[2048,256]{1,0:T(8,128)(2,1)}, bf16[2048,256]{1,0:T(8,128)(2,1)}, u32[]{:S(2)}, u32[]{:S(2)}) %collective-permute-start.128) | collective-permute-done | bytes 1048608 | tf_op jit(solution)/shard_map/ppermute | solution.py:47
  978.6 16.7 %attend_back.2 = (f32[512,1536]{1,0:T(8,128)}, bf16[512,1024]{1,0:T(8,128)(2,1)}, bf16[512,1024]{1,0:T(8,128)(2,1)}) custom-call(f32[4]{0:T(128)} %multiply_exponential_fusion.slope_ref, s32[8,512]{1,0:T(8,128)} %broadcast_in_dim.33.start_ref, bf16[512,1536]{1,0:T(8,128)(2,1)} %copy-done.50, bf16[512,1024]{1,0:T(8,128)(2,1)} %collective-permute-done.37.near_ref, ...), custom_call_target="tpu_custom_call" | custom-call | flops 4026531840 | bytes 8388608 | tf_op jit(solution)/shard_map/attend_back/pallas_call | solution.py:247
  1006.0 14.5 collective-permute-done.60.near_ref
  1144.0 20.9 %collective-permute-done.87 = bf16[256,1536]{1,0:T(8,128)(2,1)S(1)} collective-permute-done((bf16[256,1536]{1,0:T(8,128)(2,1)S(1)}, bf16[256,1536]{1,0:T(8,128)(2,1)S(1)}, u32[]{:S(2)}, u32[]{:S(2)}) %collective-permute-start.87) | collective-permute-done | bytes 786464 | tf_op jit(solution)/shard_map/ppermute | solution.py:47
  1213.1 28.0 %collective-permute-done.119 = bf16[2048,256]{1,0:T(8,128)(2,1)S(1)} collective-permute-done((bf16[2048,256]{1,0:T(8,128)(2,1)S(1)}, bf16[2048,256]{1,0:T(8,128)(2,1)S(1)}, u32[]{:S(2)}, u32[]{:S(2)}) %collective-permute-start.119) | collective-permute-done | bytes 1048608 | tf_op jit(solution)/shard_map/ppermute | solution.py:51
  1244.8 18.7 %collective-permute-done.105 = bf16[256,2048]{1,0:T(8,128)(2,1)S(1)} collective-permute-done((bf16[256,2048]{1,0:T(8,128)(2,1)S(1)}, bf16[256,2048]{1,0:T(8,128)(2,1)S(1)}, u32[]{:S(2)}, u32[]{:S(2)}) %collective-permute-start.105) | collective-permute-done | bytes 1048608 | tf_op jit(solution)/shard_map/ppermute | solution.py:51
  1293.5 15.0 collective-permute-done.104
  1316.6 14.3 collective-permute-done.117
  1337.8 14.2 collective-permute-done.103
  1365.9 16.8 %attend_back.3 = (f32[512,1536]{1,0:T(8,128)}, bf16[512,1024]{1,0:T(8,128)(2,1)}, bf16[512,1024]{1,0:T(8,128)(2,1)}) custom-call(f32[4]{0:T(128)} %multiply_exponential_fusion.slope_ref, s32[8,512]{1,0:T(8,128)} %broadcast_in_dim.33.start_ref, bf16[512,1536]{1,0:T(8,128)(2,1)} %copy-done.49, bf16[512,1024]{1,0:T(8,128)(2,1)} %collective-permute-done.7.near_ref, ...), custom_call_target="tpu_custom_call" | custom-call | flops 4026531840 | bytes 8388608 | tf_op jit(solution)/shard_map/attend_back/pallas_call | solution.py:247
  1395.8 18.4 %collective-permute-done.91 = bf16[512,256]{1,0:T(8,128)(2,1)S(1)} collective-permute-done((bf16[512,256]{1,0:T(8,128)(2,1)S(1)}, bf16[512,256]{1,0:T(8,128)(2,1)S(1)}, u32[]{:S(2)}, u32[]{:S(2)}) %collective-permute-start.91) | collective-permute-done | bytes 262176 | tf_op jit(solution)/shard_map/ppermute | solution.py:51
  1415.5 16.3 %collective-permute-done.63.far_ref = bf16[512,1024]{1,0:T(8,128)(2,1)} collective-permute-done((bf16[512,1024]{1,0:T(8,128)(2,1)}, bf16[512,1024]{1,0:T(8,128)(2,1)}, u32[]{:S(2)}, u32[]{:S(2)}) %collective-permute-start.63) | collective-permute-done | bytes 1048608 | tf_op jit(solution)/shard_map/ppermute | solution.py:136
  (871 shorter events, 912.1 us)
Async XLA Ops:
  7.3 91.7 %all-gather.9.cloned.1.call-start = ((), (), s32[]{:S(2)}) async-start(), calls=%async_computation.8 | async-start | bytes 2621440 | tf_op jit(solution)/shard_map/all_gather | solution.py:140
  14.2 101.9 %collective-permute-start.9 = (bf16[512,256]{1,0:T(8,128)(2,1)}, bf16[512,256]{1,0:T(8,128)(2,1)}, u32[]{:S(2)}, u32[]{:S(2)}) collective-permute-start(bf16[512,256]{1,0:T(8,128)(2,1)} %get-tuple-element.93), channel_id=1, source_target_pairs={{0,1},{1,0},{2,3},{3,2},{4,5},{5,4},{6,7},{7,6},{8,9},{9,8},{10,11... | collective-permute-start | bytes 786440 | tf_op jit(solution)/shard_map/ppermute | solution.py:51
  25.1 219.6 %reduce-scatter.9.cloned.1.call-start = ((), (), s32[]{:S(2)}) async-start(), calls=%async_computation.9 | async-start | bytes 2621440 | tf_op jit(solution)/shard_map/reduce_scatter | solution.py:144
  45.1 71.1 %collective-permute-start.12 = (bf16[512,256]{1,0:T(8,128)(2,1)S(1)}, bf16[512,256]{1,0:T(8,128)(2,1)}, u32[]{:S(2)}, u32[]{:S(2)}) collective-permute-start(bf16[512,256]{1,0:T(8,128)(2,1)S(1)} %collective-permute-done.10), channel_id=1, source_target_pairs={{0,6},{1,7},{2,0},{3,1},{4,2},{5,3},{6,4},{7,5},{8,14},{9,15},{10,... | collective-permute-start | bytes 786440 | tf_op jit(solution)/shard_map/ppermute | solution.py:47
  183.6 170.0 %all-gather.11.cloned.1.call-start = ((), (), s32[]{:S(2)}) async-start(), calls=%async_computation.10 | async-start | bytes 2621440 | tf_op jit(solution)/shard_map/all_gather | solution.py:140
  215.9 71.5 %collective-permute-start.19 = (bf16[256,2048]{1,0:T(8,128)(2,1)}, bf16[256,2048]{1,0:T(8,128)(2,1)S(1)}, u32[]{:S(2)}, u32[]{:S(2)}) collective-permute-start(bf16[256,2048]{1,0:T(8,128)(2,1)} %collective-permute-done.17), channel_id=1, source_target_pairs={{0,6},{1,7},{2,0},{3,1},{4,2},{5,3},{6,4},{7,5},{8,14},{9,15},{10,... | collective-permute-start | bytes 3145736 | tf_op jit(solution)/shard_map/ppermute | solution.py:47
  220.2 67.2 %collective-permute-start.18 = (bf16[256,2048]{1,0:T(8,128)(2,1)}, bf16[256,2048]{1,0:T(8,128)(2,1)}, u32[]{:S(2)}, u32[]{:S(2)}) collective-permute-start(bf16[256,2048]{1,0:T(8,128)(2,1)} %collective-permute-done.17), channel_id=1, source_target_pairs={{0,1},{1,0},{2,3},{3,2},{4,5},{5,4},{6,7},{7,6},{8,9},{9,8},{10,11... | collective-permute-start | bytes 3145736 | tf_op jit(solution)/shard_map/ppermute | solution.py:51
  249.3 155.3 %reduce-scatter.11.cloned.1.call-start = ((), (), s32[]{:S(2)}) async-start(), calls=%async_computation.11 | async-start | bytes 2621440 | tf_op jit(solution)/shard_map/reduce_scatter | solution.py:144
  287.4 64.1 %collective-permute-start.22 = (bf16[256,2048]{1,0:T(8,128)(2,1)S(1)}, bf16[256,2048]{1,0:T(8,128)(2,1)S(1)}, u32[]{:S(2)}, u32[]{:S(2)}) collective-permute-start(bf16[256,2048]{1,0:T(8,128)(2,1)S(1)} %collective-permute-done.16), channel_id=1, source_target_pairs={{0,2},{1,3},{2,4},{3,5},{4,6},{5,7},{6,0},{7,1},{8,10},{9,11},{10,... | collective-permute-start | bytes 3145736 | tf_op jit(solution)/shard_map/ppermute | solution.py:47
  372.2 105.2 %all-gather.13.cloned.1.call-start = ((), (), s32[]{:S(2)}) async-start(), calls=%async_computation.12 | async-start | bytes 2621440 | tf_op jit(solution)/shard_map/all_gather | solution.py:140
  407.6 188.1 %reduce-scatter.13.cloned.1.call-start = ((), (), s32[]{:S(2)}) async-start(), calls=%async_computation.13 | async-start | bytes 2621440 | tf_op jit(solution)/shard_map/reduce_scatter | solution.py:144
  413.6 80.6 %collective-permute-start.39 = (bf16[512,256]{1,0:T(8,128)(2,1)}, bf16[512,256]{1,0:T(8,128)(2,1)}, u32[]{:S(2)}, u32[]{:S(2)}) collective-permute-start(bf16[512,256]{1,0:T(8,128)(2,1)} %get-tuple-element.92), channel_id=1, source_target_pairs={{0,1},{1,0},{2,3},{3,2},{4,5},{5,4},{6,7},{7,6},{8,9},{9,8},{10,11... | collective-permute-start | bytes 786440 | tf_op jit(solution)/shard_map/ppermute | solution.py:51
  563.0 203.6 %all-gather.15.cloned.1.call-start = ((), (), s32[]{:S(2)}) async-start(), calls=%async_computation.14 | async-start | bytes 2621440 | tf_op jit(solution)/shard_map/all_gather | solution.py:140
  599.0 178.1 %all-gather.17.cloned.1.call-start = ((), (), s32[]{:S(2)}) async-start(), calls=%async_computation.16 | async-start | bytes 2621440 | tf_op jit(solution)/shard_map/all_gather | solution.py:140
  631.7 298.1 %reduce-scatter.17.cloned.1.call-start = ((), (), s32[]{:S(2)}) async-start(), calls=%async_computation.17 | async-start | bytes 2621440 | tf_op jit(solution)/shard_map/reduce_scatter | solution.py:144
  693.7 67.2 %collective-permute-start.52 = (bf16[256,2048]{1,0:T(8,128)(2,1)S(1)}, bf16[256,2048]{1,0:T(8,128)(2,1)S(1)}, u32[]{:S(2)}, u32[]{:S(2)}) collective-permute-start(bf16[256,2048]{1,0:T(8,128)(2,1)S(1)} %collective-permute-done.46), channel_id=1, source_target_pairs={{0,2},{1,3},{2,4},{3,5},{4,6},{5,7},{6,0},{7,1},{8,10},{9,11},{10,... | collective-permute-start | bytes 3145736 | tf_op jit(solution)/shard_map/ppermute | solution.py:47
  799.4 131.9 %reduce-scatter.15.cloned.1.call-start = ((), (), s32[]{:S(2)}) async-start(), calls=%async_computation.15 | async-start | bytes 2621440 | tf_op jit(solution)/shard_map/reduce_scatter | solution.py:144
  803.2 104.5 %collective-permute-start.125 = (bf16[2048,256]{1,0:T(8,128)(2,1)}, bf16[2048,256]{1,0:T(8,128)(2,1)}, u32[]{:S(2)}, u32[]{:S(2)}) collective-permute-start(bf16[2048,256]{1,0:T(8,128)(2,1)} %convolution_convert_fusion.9), channel_id=1, source_target_pairs={{0,1},{1,0},{2,3},{3,2},{4,5},{5,4},{6,7},{7,6},{8,9},{9,8},{10,11... | collective-permute-start | bytes 3145736 | tf_op jit(solution)/shard_map/ppermute | solution.py:51
  807.6 71.2 %collective-permute-start.126 = (bf16[2048,256]{1,0:T(8,128)(2,1)}, bf16[2048,256]{1,0:T(8,128)(2,1)}, u32[]{:S(2)}, u32[]{:S(2)}) collective-permute-start(bf16[2048,256]{1,0:T(8,128)(2,1)} %convolution_convert_fusion.8), channel_id=1, source_target_pairs={{0,1},{1,0},{2,3},{3,2},{4,5},{5,4},{6,7},{7,6},{8,9},{9,8},{10,11... | collective-permute-start | bytes 3145736 | tf_op jit(solution)/shard_map/ppermute | solution.py:51
  813.7 69.1 %collective-permute-start.109 = (bf16[256,2048]{1,0:T(8,128)(2,1)}, bf16[256,2048]{1,0:T(8,128)(2,1)}, u32[]{:S(2)}, u32[]{:S(2)}) collective-permute-start(bf16[256,2048]{1,0:T(8,128)(2,1)} %convolution_convert_fusion.19), channel_id=1, source_target_pairs={{0,6},{1,7},{2,0},{3,1},{4,2},{5,3},{6,4},{7,5},{8,14},{9,15},{10,... | collective-permute-start | bytes 3145736 | tf_op jit(solution)/shard_map/ppermute | solution.py:47
  827.2 147.1 %all-gather.19.cloned.1.call-start = ((), (), s32[]{:S(2)}) async-start(), calls=%async_computation.18 | async-start | bytes 2621440 | tf_op jit(solution)/shard_map/all_gather | solution.py:140
  882.8 181.6 %collective-permute-start.123 = (bf16[2048,256]{1,0:T(8,128)(2,1)}, bf16[2048,256]{1,0:T(8,128)(2,1)}, u32[]{:S(2)}, u32[]{:S(2)}) collective-permute-start(bf16[2048,256]{1,0:T(8,128)(2,1)} %convolution_convert_fusion.11), channel_id=1, source_target_pairs={{0,1},{1,0},{2,3},{3,2},{4,5},{5,4},{6,7},{7,6},{8,9},{9,8},{10,11... | collective-permute-start | bytes 3145736 | tf_op jit(solution)/shard_map/ppermute | solution.py:51
  936.1 166.7 %reduce-scatter.19.cloned.1.call-start = ((), (), s32[]{:S(2)}) async-start(), calls=%async_computation.19 | async-start | bytes 2621440 | tf_op jit(solution)/shard_map/reduce_scatter | solution.py:144
  967.3 97.0 %collective-permute-start.129 = (bf16[2048,256]{1,0:T(8,128)(2,1)}, bf16[2048,256]{1,0:T(8,128)(2,1)}, u32[]{:S(2)}, u32[]{:S(2)}) collective-permute-start(bf16[2048,256]{1,0:T(8,128)(2,1)} %add_convert_fusion), channel_id=1, source_target_pairs={{0,2},{1,3},{2,4},{3,5},{4,6},{5,7},{6,0},{7,1},{8,10},{9,11},{10,... | collective-permute-start | bytes 3145736 | tf_op jit(solution)/shard_map/ppermute | solution.py:47
  1050.8 117.4 %all-gather.21.cloned.1.call-start = ((), (), s32[]{:S(2)}) async-start(), calls=%async_computation.20 | async-start | bytes 2621440 | tf_op jit(solution)/shard_map/all_gather | solution.py:140
  1137.7 129.6 %reduce-scatter.21.cloned.1.call-start = ((), (), s32[]{:S(2)}) async-start(), calls=%async_computation.21 | async-start | bytes 2621440 | tf_op jit(solution)/shard_map/reduce_scatter | solution.py:144
  1188.8 172.9 %all-gather.23.cloned.1.call-start = ((), (), s32[]{:S(2)}) async-start(), calls=%async_computation.22 | async-start | bytes 2621440 | tf_op jit(solution)/shard_map/all_gather | solution.py:140
  1192.3 193.1 %collective-permute-start.116 = (bf16[2048,256]{1,0:T(8,128)(2,1)}, bf16[2048,256]{1,0:T(8,128)(2,1)}, u32[]{:S(2)}, u32[]{:S(2)}) collective-permute-start(bf16[2048,256]{1,0:T(8,128)(2,1)} %convolution_convert_fusion.15), channel_id=1, source_target_pairs={{0,1},{1,0},{2,3},{3,2},{4,5},{5,4},{6,7},{7,6},{8,9},{9,8},{10,11... | collective-permute-start | bytes 3145736 | tf_op jit(solution)/shard_map/ppermute | solution.py:51
  1196.7 68.7 %collective-permute-start.102 = (bf16[256,2048]{1,0:T(8,128)(2,1)S(1)}, bf16[256,2048]{1,0:T(8,128)(2,1)S(1)}, u32[]{:S(2)}, u32[]{:S(2)}) collective-permute-start(bf16[256,2048]{1,0:T(8,128)(2,1)S(1)} %convolution_convert_fusion.23), channel_id=1, source_target_pairs={{0,6},{1,7},{2,0},{3,1},{4,2},{5,3},{6,4},{7,5},{8,14},{9,15},{10,... | collective-permute-start | bytes 3145736 | tf_op jit(solution)/shard_map/ppermute | solution.py:47
  1242.8 65.8 %collective-permute-start.104 = (bf16[256,2048]{1,0:T(8,128)(2,1)}, bf16[256,2048]{1,0:T(8,128)(2,1)}, u32[]{:S(2)}, u32[]{:S(2)}) collective-permute-start(bf16[256,2048]{1,0:T(8,128)(2,1)} %convolution_convert_fusion.22), channel_id=1, source_target_pairs={{0,1},{1,0},{2,3},{3,2},{4,5},{5,4},{6,7},{7,6},{8,9},{9,8},{10,11... | collective-permute-start | bytes 3145736 | tf_op jit(solution)/shard_map/ppermute | solution.py:51
  1273.1 251.3 %reduce-scatter.23.cloned.1.call-start = ((), (), s32[]{:S(2)}) async-start(), calls=%async_computation.23 | async-start | bytes 2621440 | tf_op jit(solution)/shard_map/reduce_scatter | solution.py:144
  1392.7 82.7 %collective-permute-start.89 = (bf16[512,256]{1,0:T(8,128)(2,1)}, bf16[512,256]{1,0:T(8,128)(2,1)}, u32[]{:S(2)}, u32[]{:S(2)}) collective-permute-start(bf16[512,256]{1,0:T(8,128)(2,1)} %convolution_convert_fusion.40), channel_id=1, source_target_pairs={{0,1},{1,0},{2,3},{3,2},{4,5},{5,4},{6,7},{7,6},{8,9},{9,8},{10,11... | collective-permute-start | bytes 786440 | tf_op jit(solution)/shard_map/ppermute | solution.py:51
  (233 other events, 9172.9 us)
Sparse Core Ops, SparseCore 0:
  25.2 21.7 all-gather.8
  183.8 33.3 reduce-scatter.8
  249.4 20.3 all-gather.10
  372.4 32.1 reduce-scatter.10
  407.7 22.5 all-gather.12
  563.1 32.4 reduce-scatter.12
  599.1 22.5 all-gather.14
  631.8 19.7 all-gather.16
  799.5 28.6 reduce-scatter.16
  830.6 31.1 reduce-scatter.14
  936.2 23.0 all-gather.18
  1050.9 31.5 reduce-scatter.18
  1137.8 23.4 all-gather.20
  1188.9 27.6 reduce-scatter.20
  1273.2 22.8 all-gather.22
  1444.4 27.6 reduce-scatter.22
